TPU v7x, 128 devices: a whole 4x4x4 slice. The times are simulated.
128 devices in a mesh: tile: 32 (over y, x, core), sub: 4 (over z).
Axes of the slice: x: 4, y: 4, z: 4, core: 2. Of those that a mesh axis runs over, the one named last changes fastest.
Arguments:
- right_side: float32 [8, 524288], P(None, ('tile', 'sub')), may hold values from -6 to 6
- point_order: int32 [128, 4096], P(('tile', 'sub')), may hold values from 0 to 4095, each once within a row
- noise_var: float32 [524288], P(('tile', 'sub')), may hold values from 0.1 to 1
- block_pairs: int32 [12288, 2], P(('tile', 'sub')), may hold values from -1 to 2047, as said below
- pair_blocks: bfloat16 [12288, 256, 256], P(('tile', 'sub')), as said below
- diag_blocks: bfloat16 [2048, 256, 256], P(('tile', 'sub')), as said below
Outputs:
- solution: float32 [8, 524288], P(None, ('tile', 'sub'))
- residual: float32 [8, 524288], P(None, ('tile', 'sub'))
Inputs may be any that keep to these rules, and one draw needn't show every extreme that they name: `block_pairs`: the blocks form a grid of rows of 16 blocks in row-major order; device d (tile slowest, then sub) owns blocks 16 d to 16 d + 15, one grid row. A slot holds (r, c) with c the right, lower-left, lower or lower-right grid neighbour of r, or (-1, -1) when empty; every such neighbouring pair is held exactly once, by a device of the tile that owns r. On each device the live slots come first, and in every tile some device has all 96 slots live. pair_blocks[p] has the rows of block r and the columns of block c of block_pairs[p], and is zero for an empty slot; with diag_blocks these are the bfloat16 values of all nonzero blocks of a kernel matrix that is positive semi-definite before rounding. Each diag_blocks[q] is symmetric.
All inputs are finite; a program needn't handle non-finite values.
Results may differ from a plain program's by a relative error of at most 0.0075.
Values may be sent and summed in bfloat16 or wider, within the bound.
A program may use at most 64 MiB of HBM per device.

v0:
```python
import jax
import jax.numpy as jnp
from jax import lax
from jax.sharding import Mesh
from jax.sharding import PartitionSpec as P

ITERS = 3
TILE = ("tile_0", "tile_1", "tile_2")
TILE_SUB = ("tile_0", "tile_1", "tile_2", "sub")


def from_behind(block, axis, distance):
    devices = range(lax.axis_size(axis))
    route = [(i - distance, i) for i in devices if i - distance in devices]
    return lax.ppermute(block, axis, route)


def copy_for_each(array, axis):
    copies = jnp.broadcast_to(array, (lax.axis_size(axis), *array.shape))
    return lax.all_to_all(copies, axis, split_axis=0, concat_axis=0, tiled=True)


def laid_out(blocks, dim):
    shape = list(blocks.shape[1:])
    shape[dim] *= blocks.shape[0]
    return jnp.moveaxis(blocks, 0, dim).reshape(shape)


def gathered_copies(array, axis, dim):
    blocks = copy_for_each(array, axis)
    return laid_out(blocks, dim)


def split_up(array, dim, length):
    shape = array.shape
    blocks = array.reshape(*shape[:dim], length, shape[dim] // length, *shape[dim + 1 :])
    return jnp.moveaxis(blocks, dim, 0)


def sent_and_summed(array, axis, dim):
    length = lax.axis_size(axis)
    blocks = lax.all_to_all(split_up(array, dim, length), axis, 0, 0, tiled=True)
    return jnp.sum(blocks.astype(jnp.float32), axis=0)


def one_axis_at_a_time(array, axes):
    for axis in axes:
        array = lax.psum(array, axis)
    return array


def on_device(right_side, point_order, noise_var, block_pairs, pair_blocks, diag_blocks):
    sub_count = lax.axis_size("sub")
    tile_index = lax.axis_index(TILE)
    rhs_count = right_side.shape[0]
    points_dev = right_side.shape[1]
    blocks_dev = diag_blocks.shape[0]
    block_len = diag_blocks.shape[1]
    tile_blocks = blocks_dev * sub_count
    tile_points = tile_blocks * block_len
    extended = tile_blocks + blocks_dev
    first_block = tile_index * tile_blocks
    live_slot = block_pairs[:, 0] >= 0
    row_local = jnp.where(live_slot, block_pairs[:, 0] - first_block, 0)
    col_local = jnp.where(live_slot, block_pairs[:, 1] - first_block, 0)
    slot_ids = lax.broadcasted_iota(jnp.int32, (1, extended), 1)
    weight = live_slot.astype(jnp.float32)[:, None]
    row_hot = (row_local[:, None] == slot_ids).astype(jnp.float32) * weight
    col_hot = (col_local[:, None] == slot_ids).astype(jnp.float32) * weight
    curve_rhs = jnp.take(right_side, point_order[0], axis=1)

    def reduce_all(values):
        return jax.tree.map(lambda part: one_axis_at_a_time(part, TILE_SUB), values)

    solution = jnp.zeros_like(curve_rhs)
    residual = curve_rhs
    direction = curve_rhs
    norm_now = reduce_all(jnp.sum(residual * residual, axis=1))
    for iteration in range(ITERS):
        rounded = direction.astype(jnp.bfloat16)
        image_tile_rounded = gathered_copies(rounded, "sub", 1)
        ahead_row = from_behind(image_tile_rounded[:, :points_dev], TILE, -1)
        joined = jnp.concatenate([image_tile_rounded, ahead_row], axis=1).reshape(
            rhs_count, extended, block_len
        )
        from_cols = jnp.take(joined, col_local, axis=1)
        from_rows = jnp.take(joined, row_local, axis=1)
        to_rows = jnp.einsum(
            "pij,rpj->rpi", pair_blocks, from_cols, preferred_element_type=jnp.float32
        )
        to_cols = jnp.einsum(
            "pij,rpi->rpj", pair_blocks, from_rows, preferred_element_type=jnp.float32
        )
        spread = jnp.einsum("rpi,pq->rqi", to_rows, row_hot, precision=lax.Precision.HIGHEST)
        spread = spread + jnp.einsum(
            "rpj,pq->rqj", to_cols, col_hot, precision=lax.Precision.HIGHEST
        )
        spread = spread.reshape(rhs_count, extended * block_len)
        arrived = from_behind(spread[:, tile_points:].astype(jnp.bfloat16), TILE, 1).astype(
            jnp.float32
        )
        summed = sent_and_summed(
            jnp.concatenate(
                [spread[:, :points_dev] + arrived, spread[:, points_dev:tile_points]], axis=1
            ).astype(jnp.bfloat16),
            "sub",
            1,
        )
        diag_part = jnp.einsum(
            "bij,rbj->rbi",
            diag_blocks,
            rounded.reshape(rhs_count, blocks_dev, block_len),
            preferred_element_type=jnp.float32,
        )
        image_vec = summed + (
            diag_part.reshape(rhs_count, points_dev) + noise_var[None, :] * direction
        )
        curvature, cross_term, square = reduce_all(
            (
                jnp.sum(direction * image_vec, axis=1),
                jnp.sum(residual * image_vec, axis=1),
                jnp.sum(image_vec * image_vec, axis=1),
            )
        )
        step_size = norm_now / curvature
        solution = solution + step_size[:, None] * direction
        new_residual = residual - step_size[:, None] * image_vec
        if iteration + 1 < ITERS:
            norm_next = norm_now - 2.0 * step_size * cross_term + step_size * step_size * square
            direction = new_residual + (norm_next / norm_now)[:, None] * direction
            norm_now = norm_next
        residual = new_residual
    return (solution, residual)


def solution(mesh):
    torus = Mesh(
        mesh.devices.reshape(4, 4, 2, mesh.shape["sub"]), ("tile_0", "tile_1", "tile_2", "sub")
    )
    return jax.shard_map(
        on_device,
        mesh=torus,
        in_specs=(
            P(None, TILE_SUB),
            P(TILE_SUB, None),
            P(TILE_SUB),
            P(TILE_SUB, None),
            P(TILE_SUB, None, None),
            P(TILE_SUB, None, None),
        ),
        out_specs=(P(None, TILE_SUB), P(None, TILE_SUB)),
        check_vma=False,
    )
```

profile of v0, /device:TPU:0, one launch (start us, length us, event | category | flops | bytes accessed | tf_op | source)
XLA Modules:
  0.0 263.1 jit_solution(450014785858636949)
XLA Ops:
  4.4 15.7 %gather_fusion = f32[4096,8]{1,0:T(8,128)} fusion(f32[8,4096]{0,1:T(8,128)} %copy.54, s32[4096]{0:T(1024)S(1)} %broadcast_clamp_fusion), kind=kCustom, calls=%fused_computation.6 | custom fusion | bytes 278528 | tf_op jit(solution)/shard_map/jit(_take)/gather | solution.py:70
  23.7 5.4 %all-to-all-start = ((bf16[4,8,4096]{2,1,0:T(8,128)(2,1)}), bf16[4,8,4096]{2,1,0:T(8,128)(2,1)S(1)}, u32[]{:S(2)}, u32[]{:S(2)}) async-start(bf16[4,8,4096]{2,1,0:T(8,128)(2,1)} %broadcast_in_dim.53), calls=%async_computation | async-start | bytes 524288 | tf_op jit(solution)/shard_map/all_to_all | solution.py:20
  41.0 8.2 %convolution_bitcast_fusion.5 = f32[8,96,256]{2,0,1:T(8,128)S(1)} fusion(bf16[96,256,256]{2,1,0:T(8,128)(2,1)} %param.12, bf16[96,8,256]{2,1,0:T(8,128)(2,1)} %gather_fusion.1, pred[96]{0:T(512)(128)(4,1)S(1)} %get-tuple-element.56), kind=kOutput, calls=%fused_computation.12 | convolution fusion | flops 100859904 | bytes 13762656 | tf_op jit(solution)/shard_map/pij,rpj->rpi/dot_general | solution.py:88
  53.3 4.2 %collective-permute-start.1 = (bf16[8,4096]{1,0:T(8,128)(2,1)S(1)}, bf16[8,4096]{1,0:T(8,128)(2,1)S(1)}, u32[]{:S(2)}, u32[]{:S(2)}) collective-permute-start(bf16[8,4096]{1,0:T(8,128)(2,1)S(1)} %slice.79), channel_id=1, source_target_pairs={{0,4},{4,8},{8,12},{12,16},{16,20},{20,24},{24,28},{28,32},{32,36}... | collective-permute-start | bytes 196616 | tf_op jit(solution)/shard_map/ppermute | solution.py:15
  62.6 7.5 %all-to-all-done.1 = bf16[4,8,4096]{2,1,0:T(8,128)(2,1)S(1)} async-done(((bf16[4,8,4096]{2,1,0:T(8,128)(2,1)}), bf16[4,8,4096]{2,1,0:T(8,128)(2,1)S(1)}, u32[]{:S(2)}, u32[]{:S(2)}) %all-to-all-start.1) | async-done | bytes 262176 | tf_op jit(solution)/shard_map/all_to_all | solution.py:42
  71.6 14.1 %all-reduce.5 = (f32[8]{0:T(128)S(1)}, f32[8]{0:T(128)S(1)}, f32[8]{0:T(128)S(1)}) all-reduce(f32[8]{0:T(128)S(1)} %get-tuple-element.13, f32[8]{0:T(128)S(1)} %multiply_reduce_fusion.5, f32[8]{0:T(128)S(1)} %get-tuple-element.12), channel_id=1, replica_groups=mesh['tile_0'=4,'tile_1'=4,'tile_2'=2,'sub'=4] {'tile_0'}, use_global_device_ids=true, to_apply=%region_12.14 | all-reduce | flops 24 | bytes 192 | tf_op jit(solution)/shard_map/psum | solution.py:48
  85.7 7.7 %all-reduce.3 = (f32[8]{0:T(128)S(1)}, f32[8]{0:T(128)S(1)}, f32[8]{0:T(128)S(1)}) all-reduce(f32[8]{0:T(128)S(1)} %get-tuple-element.29, f32[8]{0:T(128)S(1)} %get-tuple-element.30, f32[8]{0:T(128)S(1)} %get-tuple-element.31), channel_id=1, replica_groups=mesh['tile_0'=4,'tile_1'=4,'tile_2'=2,'sub'=4] {'tile_1'}, use_global_device_ids=true, to_apply=%region_13.15 | all-reduce | flops 24 | bytes 192 | tf_op jit(solution)/shard_map/psum | solution.py:48
  95.9 8.9 %all-reduce.1 = (f32[8]{0:T(128)S(1)}, f32[8]{0:T(128)S(1)}, f32[8]{0:T(128)S(1)}) all-reduce(f32[8]{0:T(128)S(1)} %get-tuple-element.35, f32[8]{0:T(128)S(1)} %get-tuple-element.36, f32[8]{0:T(128)S(1)} %get-tuple-element.37), channel_id=1, replica_groups=mesh['tile_0'=4,'tile_1'=4,'tile_2'=2,'sub'=4] {'sub'}, use_global_device_ids=true, to_apply=%region_15.17 | all-reduce | flops 24 | bytes 192 | tf_op jit(solution)/shard_map/psum | solution.py:48
  106.1 9.1 %all_to_all.30 = bf16[4,8,4096]{2,1,0:T(8,128)(2,1)S(1)} all-to-all(bf16[4,8,4096]{2,1,0:T(8,128)(2,1)S(1)} %broadcast_in_dim.54), channel_id=1, replica_groups=mesh['tile_0'=4,'tile_1'=4,'tile_2'=2,'sub'=4] {'sub'}, dimensions={0} | all-to-all | bytes 524288 | tf_op jit(solution)/shard_map/all_to_all | solution.py:20
  119.6 7.9 %convolution_bitcast_fusion.3 = f32[8,96,256]{2,0,1:T(8,128)S(1)} fusion(bf16[96,256,256]{2,1,0:T(8,128)(2,1)} %param.12, bf16[96,8,256]{2,1,0:T(8,128)(2,1)S(1)} %gather_fusion.3, pred[96]{0:T(512)(128)(4,1)S(1)} %get-tuple-element.56), kind=kOutput, calls=%fused_computation.10 | convolution fusion | flops 100859904 | bytes 13762656 | tf_op jit(solution)/shard_map/pij,rpj->rpi/dot_general | solution.py:88
  128.5 6.4 %convolution_bitcast_fusion.2 = f32[8,96,256]{2,0,1:T(8,128)S(1)} fusion(bf16[96,256,256]{2,1,0:T(8,128)(2,1)} %param.12, bf16[96,8,256]{2,1,0:T(8,128)(2,1)S(1)} %gather_fusion.4, pred[96]{0:T(512)(128)(4,1)S(1)} %get-tuple-element.50), kind=kOutput, calls=%fused_computation.9 | convolution fusion | flops 100859904 | bytes 13762656 | tf_op jit(solution)/shard_map/pij,rpi->rpj/dot_general | solution.py:91
  136.3 4.7 %collective-permute-start.3 = (bf16[8,4096]{1,0:T(8,128)(2,1)S(1)}, bf16[8,4096]{1,0:T(8,128)(2,1)S(1)}, u32[]{:S(2)}, u32[]{:S(2)}) collective-permute-start(bf16[8,4096]{1,0:T(8,128)(2,1)S(1)} %slice.83), channel_id=1, source_target_pairs={{0,4},{4,8},{8,12},{12,16},{16,20},{20,24},{24,28},{28,32},{32,36}... | collective-permute-start | bytes 196616 | tf_op jit(solution)/shard_map/ppermute | solution.py:15
  141.9 9.9 %all_to_all.31 = bf16[4,8,4096]{2,1,0:T(8,128)(2,1)S(1)} all-to-all(bf16[4,8,4096]{2,1,0:T(8,128)(2,1)S(1)} %bitcast.171), channel_id=1, replica_groups=mesh['tile_0'=4,'tile_1'=4,'tile_2'=2,'sub'=4] {'sub'}, dimensions={0} | all-to-all | bytes 524288 | tf_op jit(solution)/shard_map/all_to_all | solution.py:42
  153.4 9.7 %all-reduce.4 = (f32[8]{0:T(128)S(1)}, f32[8]{0:T(128)S(1)}, f32[8]{0:T(128)S(1)}) all-reduce(f32[8]{0:T(128)S(1)} %get-tuple-element.11, f32[8]{0:T(128)S(1)} %get-tuple-element.10, f32[8]{0:T(128)S(1)} %get-tuple-element.9), channel_id=1, replica_groups=mesh['tile_0'=4,'tile_1'=4,'tile_2'=2,'sub'=4] {'tile_0'}, use_global_device_ids=true, to_apply=%region_28.30 | all-reduce | flops 24 | bytes 192 | tf_op jit(solution)/shard_map/psum | solution.py:48
  163.1 7.7 %all-reduce.2 = (f32[8]{0:T(128)S(1)}, f32[8]{0:T(128)S(1)}, f32[8]{0:T(128)S(1)}) all-reduce(f32[8]{0:T(128)S(1)} %get-tuple-element.26, f32[8]{0:T(128)S(1)} %get-tuple-element.27, f32[8]{0:T(128)S(1)} %get-tuple-element.28), channel_id=1, replica_groups=mesh['tile_0'=4,'tile_1'=4,'tile_2'=2,'sub'=4] {'tile_1'}, use_global_device_ids=true, to_apply=%region_29.31 | all-reduce | flops 24 | bytes 192 | tf_op jit(solution)/shard_map/psum | solution.py:48
  173.3 8.9 %all-reduce = (f32[8]{0:T(128)S(1)}, f32[8]{0:T(128)S(1)}, f32[8]{0:T(128)S(1)}) all-reduce(f32[8]{0:T(128)S(1)} %get-tuple-element.32, f32[8]{0:T(128)S(1)} %get-tuple-element.33, f32[8]{0:T(128)S(1)} %get-tuple-element.34), channel_id=1, replica_groups=mesh['tile_0'=4,'tile_1'=4,'tile_2'=2,'sub'=4] {'sub'}, use_global_device_ids=true, to_apply=%region_31.33 | all-reduce | flops 24 | bytes 192 | tf_op jit(solution)/shard_map/psum | solution.py:48
  184.1 9.1 %all_to_all.32 = bf16[4,8,4096]{2,1,0:T(8,128)(2,1)S(1)} all-to-all(bf16[4,8,4096]{2,1,0:T(8,128)(2,1)S(1)} %broadcast_in_dim.55), channel_id=1, replica_groups=mesh['tile_0'=4,'tile_1'=4,'tile_2'=2,'sub'=4] {'sub'}, dimensions={0} | all-to-all | bytes 524288 | tf_op jit(solution)/shard_map/all_to_all | solution.py:20
  197.7 7.9 %convolution_bitcast_fusion.1 = f32[8,96,256]{2,0,1:T(8,128)S(1)} fusion(bf16[96,256,256]{2,1,0:T(8,128)(2,1)} %param.12, bf16[96,8,256]{2,1,0:T(8,128)(2,1)S(1)} %gather_fusion.5, pred[96]{0:T(512)(128)(4,1)S(1)} %get-tuple-element.56), kind=kOutput, calls=%fused_computation.8 | convolution fusion | flops 100859904 | bytes 13762656 | tf_op jit(solution)/shard_map/pij,rpj->rpi/dot_general | solution.py:88
  206.6 6.4 %convolution_bitcast_fusion = f32[8,96,256]{2,0,1:T(8,128)S(1)} fusion(bf16[96,256,256]{2,1,0:T(8,128)(2,1)} %param.12, bf16[96,8,256]{2,1,0:T(8,128)(2,1)S(1)} %gather_fusion.6, pred[96]{0:T(512)(128)(4,1)S(1)} %get-tuple-element.50), kind=kOutput, calls=%fused_computation.7 | convolution fusion | flops 100859904 | bytes 13762656 | tf_op jit(solution)/shard_map/pij,rpi->rpj/dot_general | solution.py:91
  214.4 4.7 %collective-permute-start.5 = (bf16[8,4096]{1,0:T(8,128)(2,1)S(1)}, bf16[8,4096]{1,0:T(8,128)(2,1)S(1)}, u32[]{:S(2)}, u32[]{:S(2)}) collective-permute-start(bf16[8,4096]{1,0:T(8,128)(2,1)S(1)} %slice.87), channel_id=1, source_target_pairs={{0,4},{4,8},{8,12},{12,16},{16,20},{20,24},{24,28},{28,32},{32,36}... | collective-permute-start | bytes 196616 | tf_op jit(solution)/shard_map/ppermute | solution.py:15
  220.1 9.9 %all_to_all.33 = bf16[4,8,4096]{2,1,0:T(8,128)(2,1)S(1)} all-to-all(bf16[4,8,4096]{2,1,0:T(8,128)(2,1)S(1)} %bitcast.172), channel_id=1, replica_groups=mesh['tile_0'=4,'tile_1'=4,'tile_2'=2,'sub'=4] {'sub'}, dimensions={0} | all-to-all | bytes 524288 | tf_op jit(solution)/shard_map/all_to_all | solution.py:42
  230.9 11.5 %psum.232 = f32[8]{0:T(128)S(1)} all-reduce(f32[8]{0:T(128)S(1)} %get-tuple-element.60), channel_id=1, replica_groups=mesh['tile_0'=4,'tile_1'=4,'tile_2'=2,'sub'=4] {'tile_0'}, use_global_device_ids=true, to_apply=%region_34.36 | all-reduce | flops 8 | bytes 64 | tf_op jit(solution)/shard_map/psum | solution.py:48
  242.4 7.7 %psum.233 = f32[8]{0:T(128)S(1)} all-reduce(f32[8]{0:T(128)S(1)} %psum.232), channel_id=1, replica_groups=mesh['tile_0'=4,'tile_1'=4,'tile_2'=2,'sub'=4] {'tile_1'}, use_global_device_ids=true, to_apply=%region_35.37 | all-reduce | flops 8 | bytes 64 | tf_op jit(solution)/shard_map/psum | solution.py:48
  252.5 8.9 %psum.235 = f32[8]{0:T(128)S(1)} all-reduce(f32[8]{0:T(128)S(1)} %psum.234), channel_id=1, replica_groups=mesh['tile_0'=4,'tile_1'=4,'tile_2'=2,'sub'=4] {'sub'}, use_global_device_ids=true, to_apply=%region_37.39 | all-reduce | flops 8 | bytes 64 | tf_op jit(solution)/shard_map/psum | solution.py:48
  (105 shorter events, 59.7 us)
Async XLA Ops:
  0.6 69.5 %copy-start = (bf16[16,256,256]{2,1,0:T(8,128)(2,1)S(1)}, bf16[16,256,256]{2,1,0:T(8,128)(2,1)}, u32[]{:S(2)}) copy-start(bf16[16,256,256]{2,1,0:T(8,128)(2,1)} %param.13) | copy-start | bytes 6291460
  23.7 12.1 %all-to-all-start = ((bf16[4,8,4096]{2,1,0:T(8,128)(2,1)}), bf16[4,8,4096]{2,1,0:T(8,128)(2,1)S(1)}, u32[]{:S(2)}, u32[]{:S(2)}) async-start(bf16[4,8,4096]{2,1,0:T(8,128)(2,1)} %broadcast_in_dim.53), calls=%async_computation | async-start | bytes 524288 | tf_op jit(solution)/shard_map/all_to_all | solution.py:20
  35.8 3.1 %collective-permute-start = (bf16[8,4096]{1,0:T(8,128)(2,1)S(1)}, bf16[8,4096]{1,0:T(8,128)(2,1)S(1)}, u32[]{:S(2)}, u32[]{:S(2)}) collective-permute-start(bf16[8,4096]{1,0:T(8,128)(2,1)S(1)} %slice.77), channel_id=1, source_target_pairs={{4,0},{8,4},{12,8},{16,12},{20,16},{24,20},{28,24},{32,28},{36,32}... | collective-permute-start | bytes 196616 | tf_op jit(solution)/shard_map/ppermute | solution.py:15
  37.1 81.8 %copy-start.9 = (s32[1024]{0:T(1024)}, s32[1024]{0:T(1024)S(1)}, u32[]{:S(2)}) copy-start(s32[1024]{0:T(1024)S(1)} %pad_clamp_fusion) | copy-start | bytes 12292
  41.0 9.1 %copy-start.1 = (bf16[96,256,256]{2,1,0:T(8,128)(2,1)S(1)}, bf16[96,256,256]{2,1,0:T(8,128)(2,1)}, u32[]{:S(2)}) copy-start(bf16[96,256,256]{2,1,0:T(8,128)(2,1)} %param.12) | copy-start | bytes 37748740
  50.1 55.2 %copy-start.8 = (f32[4096]{0:T(1024)S(1)}, f32[4096]{0:T(1024)}, u32[]{:S(2)}) copy-start(f32[4096]{0:T(1024)} %param.10) | copy-start | bytes 49156
  53.3 5.1 %collective-permute-start.1 = (bf16[8,4096]{1,0:T(8,128)(2,1)S(1)}, bf16[8,4096]{1,0:T(8,128)(2,1)S(1)}, u32[]{:S(2)}, u32[]{:S(2)}) collective-permute-start(bf16[8,4096]{1,0:T(8,128)(2,1)S(1)} %slice.79), channel_id=1, source_target_pairs={{0,4},{4,8},{8,12},{12,16},{16,20},{20,24},{24,28},{28,32},{32,36}... | collective-permute-start | bytes 196616 | tf_op jit(solution)/shard_map/ppermute | solution.py:15
  59.1 10.9 %all-to-all-start.1 = ((bf16[4,8,4096]{2,1,0:T(8,128)(2,1)}), bf16[4,8,4096]{2,1,0:T(8,128)(2,1)S(1)}, u32[]{:S(2)}, u32[]{:S(2)}) async-start(bf16[4,8,4096]{2,1,0:T(8,128)(2,1)} %bitcast.20), calls=%async_computation.1 | async-start | bytes 524288 | tf_op jit(solution)/shard_map/all_to_all | solution.py:42
  71.6 34.5 %copy-start.3 = (f32[16,8,256]{2,1,0:T(8,128)}, f32[16,8,256]{2,1,0:T(8,128)S(1)}, u32[]{:S(2)}) copy-start(f32[16,8,256]{2,1,0:T(8,128)S(1)} %get-tuple-element.58) | copy-start | bytes 393220
  115.2 3.1 %collective-permute-start.2 = (bf16[8,4096]{1,0:T(8,128)(2,1)S(1)}, bf16[8,4096]{1,0:T(8,128)(2,1)S(1)}, u32[]{:S(2)}, u32[]{:S(2)}) collective-permute-start(bf16[8,4096]{1,0:T(8,128)(2,1)S(1)} %slice.81), channel_id=1, source_target_pairs={{4,0},{8,4},{12,8},{16,12},{20,16},{24,20},{28,24},{32,28},{36,32}... | collective-permute-start | bytes 196616 | tf_op jit(solution)/shard_map/ppermute | solution.py:15
  128.5 23.5 %copy-start.5 = (f32[8,16,256]{2,0,1:T(8,128)S(1)}, f32[8,16,256]{2,0,1:T(8,128)}, u32[]{:S(2)}) copy-start(f32[8,16,256]{2,0,1:T(8,128)} %get-tuple-element.49) | copy-start | bytes 393220
  128.5 54.9 %copy-start.2 = (f32[8,4096]{1,0:T(8,128)S(1)}, f32[8,4096]{1,0:T(8,128)}, u32[]{:S(2)}) copy-start(f32[8,4096]{1,0:T(8,128)} %get-tuple-element.45) | copy-start | bytes 393220
  128.5 54.9 %copy-start.4 = (f32[16,8,256]{2,1,0:T(8,128)S(1)}, f32[16,8,256]{2,1,0:T(8,128)}, u32[]{:S(2)}) copy-start(f32[16,8,256]{2,1,0:T(8,128)} %copy-done.3) | copy-start | bytes 393220
  136.3 5.6 %collective-permute-start.3 = (bf16[8,4096]{1,0:T(8,128)(2,1)S(1)}, bf16[8,4096]{1,0:T(8,128)(2,1)S(1)}, u32[]{:S(2)}, u32[]{:S(2)}) collective-permute-start(bf16[8,4096]{1,0:T(8,128)(2,1)S(1)} %slice.83), channel_id=1, source_target_pairs={{0,4},{4,8},{8,12},{12,16},{16,20},{20,24},{24,28},{28,32},{32,36}... | collective-permute-start | bytes 196616 | tf_op jit(solution)/shard_map/ppermute | solution.py:15
  193.2 3.1 %collective-permute-start.4 = (bf16[8,4096]{1,0:T(8,128)(2,1)S(1)}, bf16[8,4096]{1,0:T(8,128)(2,1)S(1)}, u32[]{:S(2)}, u32[]{:S(2)}) collective-permute-start(bf16[8,4096]{1,0:T(8,128)(2,1)S(1)} %slice.85), channel_id=1, source_target_pairs={{4,0},{8,4},{12,8},{16,12},{20,16},{24,20},{28,24},{32,28},{36,32}... | collective-permute-start | bytes 196616 | tf_op jit(solution)/shard_map/ppermute | solution.py:15
  206.6 23.5 %copy-start.6 = (f32[8,16,256]{2,0,1:T(8,128)S(1)}, f32[8,16,256]{2,0,1:T(8,128)}, u32[]{:S(2)}) copy-start(f32[8,16,256]{2,0,1:T(8,128)} %get-tuple-element.49) | copy-start | bytes 393220
  206.6 23.5 %copy-start.7 = (f32[8,16,256]{2,0,1:T(8,128)S(1)}, f32[8,16,256]{2,0,1:T(8,128)}, u32[]{:S(2)}) copy-start(f32[8,16,256]{2,0,1:T(8,128)} %get-tuple-element.43) | copy-start | bytes 393220
  206.6 54.8 %copy-start.10 = (f32[8]{0:T(128)S(1)}, f32[8]{0:T(128)}, u32[]{:S(2)}) copy-start(f32[8]{0:T(128)} %get-tuple-element.41) | copy-start | bytes 100
  214.4 5.6 %collective-permute-start.5 = (bf16[8,4096]{1,0:T(8,128)(2,1)S(1)}, bf16[8,4096]{1,0:T(8,128)(2,1)S(1)}, u32[]{:S(2)}, u32[]{:S(2)}) collective-permute-start(bf16[8,4096]{1,0:T(8,128)(2,1)S(1)} %slice.87), channel_id=1, source_target_pairs={{0,4},{4,8},{8,12},{12,16},{16,20},{20,24},{24,28},{28,32},{32,36}... | collective-permute-start | bytes 196616 | tf_op jit(solution)/shard_map/ppermute | solution.py:15
where the time goes:
time: 265 us; the launch traced here: 263 us
  blocking collectives  131 us (49%)
  matrix products  47.9 us (18%)
  local copies, waits for them, and re-layouts  28.7 us (11%)
  starting transfers between devices  26.8 us (10%)
  waiting for transfers between devices  17.6 us (7%)
  other arithmetic  10.6 us (4%)
    psum x12, blocking collectives, one_axis_at_a_time(): array = lax.psum(array, axis)  92.5 us
    dot_general x3, matrix products, on_device(): jnp.einsum('pij,rpj->rpi', pair_blocks, from_cols, preferred_element_type...  24.1 us
    all_to_all x2, blocking collectives, sent_and_summed(): lax.all_to_all(split_up(array, dim, length), axis, 0, 0, tiled=True)  19.9 us
    all_to_all x2, blocking collectives, copy_for_each(): return lax.all_to_all(copies, axis, split_axis=0, concat_axis=0, tiled=True)  18.1 us
    ppermute x6, starting transfers between devices, from_behind(): return lax.ppermute(block, axis, route)  17.9 us
    gather x2, local copies, waits for them, and re-layouts, on_device(): curve_rhs = jnp.take(right_side, point_order[0], axis=1)  17.8 us
    dot_general x3, matrix products, on_device(): jnp.einsum('pij,rpi->rpj', pair_blocks, from_rows, preferred_element_type...  14.5 us
    ppermute x6, waiting for transfers between devices, from_behind(): return lax.ppermute(block, axis, route)  7.55 us
  transfers between devices with their start and end apart: 8, of which 8 were waited for; matrix products, arithmetic and copies ran while one was open for 2% of the time, Pallas kernels for 0%

commit v1 on v0

v1 whole, which is shorter than its diff:
```python
import functools
import math

import jax
import jax.numpy as jnp
from jax import lax
from jax.experimental import pallas as pl
from jax.experimental.pallas import tpu as pltpu
from jax.sharding import PartitionSpec as P

ITERS = 3
UNROLL = 32
PARTS = 6
F32 = jnp.float32
BF16 = jnp.bfloat16
MESH = pl.DeviceIdType.MESH


def kernel(
    cfg,
    right_hbm,
    order_hbm,
    noise_hbm,
    pairs_hbm,
    blocks_hbm,
    diag_hbm,
    sol_ref,
    res_ref,
    right,
    order,
    noise,
    pairs,
    blocks,
    diag,
    base,
    image,
    twice,
    resid,
    direct,
    image_next,
    resid_image,
    diag_part,
    field,
    products,
    partial,
    arrived,
    ahead,
    table_vec,
    table,
    sums,
    in_sem,
    blocks_sem,
    table_sem,
    field_send,
    field_recv,
    field_fwd,
    ahead_send,
    ahead_recv,
    part_send,
    part_recv,
    part_ahead_send,
    part_ahead_recv,
    sums_send,
    sums_recv,
):
    tiles, subs, side, blk_dev, block, slots, rhs = cfg
    half = blk_dev // 2
    t = lax.axis_index("tile")
    s = lax.axis_index("sub")
    core = lax.rem(t, 2)
    chip_x = lax.rem(t // 2, side)
    chip_y = t // (2 * side)
    above = lax.rem(s + 1, subs)
    below = lax.rem(s + subs - 1, subs)
    across = lax.rem(s + 2, subs)
    has_behind = t > 0
    has_ahead = t < tiles - 1

    loads = [
        pltpu.make_async_copy(right_hbm, right, in_sem.at[0]),
        pltpu.make_async_copy(order_hbm, order, in_sem.at[1]),
        pltpu.make_async_copy(pairs_hbm, pairs, in_sem.at[2]),
        pltpu.make_async_copy(noise_hbm, noise, in_sem.at[3]),
        pltpu.make_async_copy(diag_hbm, diag, in_sem.at[4]),
    ]
    step = slots // PARTS
    block_loads = [
        pltpu.make_async_copy(
            blocks_hbm.at[pl.ds(i * step, step)],
            blocks.at[pl.ds(i * step, step)],
            blocks_sem.at[i],
        )
        for i in range(PARTS)
    ]

    group1 = core * subs + s

    def partner1(index):
        return (t - core + index // subs, lax.rem(index, subs))

    def partner2(index):
        return ((chip_y * side + index) * 2 + core, s)

    def partner3(index):
        return ((index * side + chip_x) * 2 + core, s)

    stages = (
        (2 * subs, group1, partner1, 0),
        (side, chip_x, partner2, 2 * subs),
        (side, chip_y, partner3, 2 * subs + side),
    )

    barrier = pltpu.get_barrier_semaphore()
    greeted = 0
    for count, mine, partner, unused in stages:
        for j in range(1, count):
            pl.semaphore_signal(
                barrier, inc=1, device_id=partner(lax.rem(mine + j, count)), device_id_type=MESH
            )
            greeted += 1
    far_ahead = (core == 1) & has_ahead
    far_behind = (core == 0) & has_behind

    @pl.when(far_ahead)
    def _():
        pl.semaphore_signal(barrier, inc=1, device_id=(t + 1, s), device_id_type=MESH)

    @pl.when(far_behind)
    def _():
        pl.semaphore_signal(barrier, inc=1, device_id=(t - 1, s), device_id_type=MESH)

    for copy in loads:
        copy.start()
    for copy in block_loads:
        copy.start()

    loads[0].wait()
    loads[1].wait()
    lanes = 128
    chunks = right.shape[1] // lanes

    def permute(i, carry):
        at = pl.multiple_of(i * lanes, lanes)
        index = jnp.broadcast_to(order[:, pl.ds(at, lanes)], (rhs, lanes))
        low = lax.bitwise_and(index, lanes - 1)
        high = lax.shift_right_logical(index, 7)
        out = jnp.zeros((rhs, lanes), F32)
        for h in range(chunks):
            picked = jnp.take_along_axis(right[:, h * lanes : (h + 1) * lanes], low, axis=1)
            out = jnp.where(high == h, picked, out)
        base[:, pl.ds(at, lanes)] = out
        return carry

    lax.fori_loop(0, chunks, permute, 0)

    def put_field(k, values):
        for b in range(blk_dev):
            field[k, s * blk_dev + b] = values[:, b * block : (b + 1) * block].astype(BF16)

    def field_half(k, row, h):
        return field.at[k, pl.ds(row * blk_dev + h * half, half)]

    def field_copy(k, row, h, target, send):
        return pltpu.make_async_remote_copy(
            src_ref=field_half(k, row, h),
            dst_ref=field_half(k, row, h),
            send_sem=send,
            recv_sem=field_recv.at[k, row, h],
            device_id=(t, target),
            device_id_type=MESH,
        )

    def ahead_copy(k, h):
        return pltpu.make_async_remote_copy(
            src_ref=field_half(k, 0, h),
            dst_ref=field_half(k, subs, h),
            send_sem=ahead_send.at[k, h],
            recv_sem=ahead_recv.at[k, h],
            device_id=(t - 1, s),
            device_id_type=MESH,
        )

    def pass_back(k, row, h):
        @pl.when((row == 0) & has_behind)
        def _():
            ahead_copy(k, h).start()

    def start_field(k):
        for target, h, n in ((above, 0, 0), (below, 1, 1), (above, 1, 2), (below, 0, 3)):
            field_copy(k, s, h, target, field_send.at[k, n]).start()
        for h in range(2):
            pass_back(k, s, h)

    def finish_field(k):
        field_copy(k, below, 0, s, field_send.at[k, 0]).wait_recv()
        field_copy(k, below, 0, above, field_fwd.at[k, 0]).start()
        pass_back(k, below, 0)
        field_copy(k, above, 1, s, field_send.at[k, 0]).wait_recv()
        field_copy(k, above, 1, below, field_fwd.at[k, 1]).start()
        pass_back(k, above, 1)
        for row, h in ((below, 1), (above, 0), (across, 0), (across, 1)):
            field_copy(k, row, h, s, field_send.at[k, 0]).wait_recv()
            pass_back(k, row, h)

        @pl.when(has_ahead)
        def _():
            for h in range(2):
                ahead_copy(k, h).wait_recv()

    def drain_field(k):
        for target, h, n in ((above, 0, 0), (below, 1, 1), (above, 1, 2), (below, 0, 3)):
            field_copy(k, s, h, target, field_send.at[k, n]).wait_send()
        field_copy(k, below, 0, above, field_fwd.at[k, 0]).wait_send()
        field_copy(k, above, 1, below, field_fwd.at[k, 1]).wait_send()

        @pl.when(has_behind)
        def _():
            for h in range(2):
                ahead_copy(k, h).wait_send()

    def sums_copy(k, stage, j):
        count, mine, partner, offset = stages[stage]
        other = lax.rem(mine + j, count)
        return pltpu.make_async_remote_copy(
            src_ref=sums.at[k, offset + mine],
            dst_ref=sums.at[k, offset + mine],
            send_sem=sums_send.at[k, offset + j],
            recv_sem=sums_recv.at[k, offset + mine],
            device_id=partner(other),
            device_id_type=MESH,
        )

    def sums_start(k, stage, values):
        count, mine, partner, offset = stages[stage]
        sums[k, offset + mine] = values
        for j in range(1, count):
            sums_copy(k, stage, j).start()

    def sums_finish(k, stage):
        count, mine, partner, offset = stages[stage]
        for j in range(1, count):
            other = lax.rem(mine + j, count)
            pltpu.make_async_remote_copy(
                src_ref=sums.at[k, offset + other],
                dst_ref=sums.at[k, offset + other],
                send_sem=sums_send.at[k, offset + j],
                recv_sem=sums_recv.at[k, offset + other],
                device_id=partner(other),
                device_id_type=MESH,
            ).wait_recv()
        total = sums[k, offset]
        for j in range(1, count):
            total = total + sums[k, offset + j]
        return total

    def sums_drain(k):
        for stage in range(3):
            for j in range(1, stages[stage][0]):
                sums_copy(k, stage, j).wait_send()

    def fold(values):
        parts = [values[:, i * lanes : (i + 1) * lanes] for i in range(chunks)]
        while len(parts) > 1:
            parts = [a + b for a, b in zip(parts[::2], parts[1::2])]
        return parts[0]

    def pack(*values):
        folded = [fold(v) for v in values]
        while len(folded) < 3:
            folded.append(jnp.zeros_like(folded[0]))
        return jnp.stack(folded)

    def scalar(total, n):
        return jnp.sum(total[n], axis=1, keepdims=True)

    first = t * (subs * blk_dev)

    def row_of(p):
        return jnp.maximum(pairs[0, p] - first, 0)

    def col_of(p):
        return jnp.maximum(pairs[1, p] - first, 0)

    def build_table():
        shape = (8, lanes)
        ids = lax.broadcasted_iota(jnp.int32, shape, 0) * lanes + lax.broadcasted_iota(
            jnp.int32, shape, 1
        )

        def add_slot(i, found):
            for u in range(8):
                p = i * 8 + u
                row = pairs[0, p]
                col = pairs[1, p]
                apart = col - row
                kind = jnp.where(apart == 1, 0, apart - (blk_dev - 2))
                live = row >= 0
                key_col = jnp.where(live, (col - first) * 8 + kind, -1)
                key_row = jnp.where(live, (row - first) * 8 + 4 + kind, -1)
                found = jnp.where(ids == key_col, p + 1, found)
                found = jnp.where(ids == key_row, p + 1 + slots, found)
            return found

        table_vec[...] = lax.fori_loop(0, slots // 8, add_slot, jnp.zeros(shape, jnp.int32))
        move = pltpu.make_async_copy(table_vec, table, table_sem)
        move.start()
        move.wait()
        products[0] = jnp.zeros((rhs, block), F32)

    def diag_products(k):
        def body(i, carry):
            for u in range(4):
                b = i * 4 + u
                at = pl.multiple_of(b * block, block)
                diag_part[:, pl.ds(at, block)] = jnp.dot(
                    field[k, s * blk_dev + b], diag[b], preferred_element_type=F32
                )
            return carry

        lax.fori_loop(0, blk_dev // 4, body, 0)

    def pair_products(k, low, high):
        def body(i, carry):
            for u in range(UNROLL):
                p = i * UNROLL + u
                kernel_block = blocks[p]
                products[1 + p] = lax.dot_general(
                    field[k, row_of(p)],
                    kernel_block,
                    (((1,), (0,)), ((), ())),
                    preferred_element_type=F32,
                )
                products[1 + slots + p] = lax.dot_general(
                    field[k, col_of(p)],
                    kernel_block,
                    (((1,), (1,)), ((), ())),
                    preferred_element_type=F32,
                )
            return carry

        lax.fori_loop(low, high, body, 0)

    def gathered_sum(row, b):
        at = (row * blk_dev + b) * 8
        total = products[table[at // lanes, lax.rem(at, lanes)]]
        for n in range(1, 8):
            total = total + products[table[at // lanes, lax.rem(at, lanes) + n]]
        return total

    def fill_partial(k, row, n, with_ahead):
        def body(i, carry):
            for u in range(4):
                b = i * 4 + u
                total = gathered_sum(row, b)
                if with_ahead:
                    total = total + jnp.where(row == 0, ahead[k, b].astype(F32), 0.0)
                partial[k, n, b] = total.astype(BF16)
            return carry

        lax.fori_loop(0, blk_dev // 4, body, 0)

    def part_copy(k, n, row):
        return pltpu.make_async_remote_copy(
            src_ref=partial.at[k, n],
            dst_ref=arrived.at[k, s],
            send_sem=part_send.at[k, n],
            recv_sem=part_recv.at[k, s],
            device_id=(t, row),
            device_id_type=MESH,
        )

    def part_ahead_copy(k):
        return pltpu.make_async_remote_copy(
            src_ref=partial.at[k, 3],
            dst_ref=ahead.at[k],
            send_sem=part_ahead_send.at[k],
            recv_sem=part_ahead_recv.at[k],
            device_id=(t + 1, s),
            device_id_type=MESH,
        )

    rows = (
        jnp.where(s == 1, 2, 1),
        jnp.where((s == 0) | (s == 3), 2, 3),
        jnp.where(s == 0, 3, 0),
    )

    def send_products(k):
        @pl.when(has_ahead)
        def _():
            fill_partial(k, subs, 3, False)
            part_ahead_copy(k).start()

        for n in range(2):
            fill_partial(k, rows[n], n, False)
            part_copy(k, n, rows[n]).start()

        @pl.when(has_behind)
        def _():
            part_ahead_copy(k).wait_recv()

        fill_partial(k, rows[2], 2, True)
        part_copy(k, 2, rows[2]).start()

    def take_products(k, vector, out):
        own = jnp.where(s == 0, 1.0, 0.0).astype(F32)

        def body(i, carry):
            for u in range(4):
                b = i * 4 + u
                at = pl.ds(pl.multiple_of(b * block, block), block)
                total = gathered_sum(s, b) + diag_part[:, at]
                diag_part[:, at] = total + jnp.where(s == 0, ahead[k, b].astype(F32), 0.0)
            return carry

        lax.fori_loop(0, blk_dev // 4, body, 0)
        for j in range(1, subs):
            other = lax.rem(s + j, subs)
            pltpu.make_async_remote_copy(
                src_ref=partial.at[k, 0],
                dst_ref=arrived.at[k, other],
                send_sem=part_send.at[k, 0],
                recv_sem=part_recv.at[k, other],
                device_id=(t, other),
                device_id_type=MESH,
            ).wait_recv()
        others = [lax.rem(s + j, subs) for j in range(1, subs)]

        def combine(i, carry):
            for u in range(4):
                b = i * 4 + u
                at = pl.ds(pl.multiple_of(b * block, block), block)
                total = arrived[k, others[0], b].astype(F32)
                for other in others[1:]:
                    total = total + arrived[k, other, b].astype(F32)
                out[:, at] = total + (diag_part[:, at] + noise[:, at] * vector[:, at])
            return carry

        lax.fori_loop(0, blk_dev // 4, combine, 0)

    def drain_products(k):
        for n in range(3):
            part_copy(k, n, rows[n]).wait_send()

        @pl.when(has_ahead)
        def _():
            part_ahead_copy(k).wait_send()

    trips = slots // UNROLL

    put_field(0, base[...])

    @pl.when(jnp.logical_not(has_ahead))
    def _():
        for k in range(ITERS):
            for b in range(blk_dev):
                field[k, subs * blk_dev + b] = jnp.zeros((rhs, block), BF16)

    @pl.when(jnp.logical_not(has_behind))
    def _():
        for k in range(ITERS):
            ahead[k] = jnp.zeros((blk_dev, rhs, block), BF16)

    pl.semaphore_wait(barrier, greeted + jnp.where(far_ahead | far_behind, 1, 0))
    start_field(0)
    loads[2].wait()
    build_table()
    loads[4].wait()
    diag_products(0)
    finish_field(0)
    for copy in block_loads:
        copy.wait()
    pair_products(0, 0, trips)
    send_products(0)
    loads[3].wait()
    take_products(0, base, image)

    b_now = base[...]
    q_now = image[...]
    put_field(1, q_now)
    start_field(1)
    sums_start(0, 0, pack(b_now * b_now, b_now * q_now, q_now * q_now))
    diag_products(1)
    finish_field(1)
    sums_start(0, 1, sums_finish(0, 0))
    pair_products(1, 0, 1)
    sums_start(0, 2, sums_finish(0, 1))
    pair_products(1, 1, trips)
    send_products(1)
    total = sums_finish(0, 2)
    norm0 = scalar(total, 0)
    curve0 = scalar(total, 1)
    square0 = scalar(total, 2)
    step0 = norm0 / curve0
    norm1 = norm0 - 2.0 * step0 * curve0 + step0 * step0 * square0
    mix0 = norm1 / norm0
    resid[...] = base[...] - step0 * image[...]
    direct[...] = resid[...] + mix0 * base[...]
    take_products(1, image, twice)
    resid_image[...] = image[...] - step0 * twice[...]
    image_next[...] = resid_image[...] + mix0 * image[...]

    put_field(2, image_next[...])
    start_field(2)
    q_now = image_next[...]
    sums_start(1, 0, pack(direct[...] * q_now, resid[...] * q_now, q_now * q_now))
    diag_products(2)
    finish_field(2)
    sums_start(1, 1, sums_finish(1, 0))
    pair_products(2, 0, 1)
    sums_start(1, 2, sums_finish(1, 1))
    pair_products(2, 1, trips)
    send_products(2)
    total = sums_finish(1, 2)
    curve1 = scalar(total, 0)
    cross1 = scalar(total, 1)
    square1 = scalar(total, 2)
    step1 = norm1 / curve1
    norm2 = norm1 - 2.0 * step1 * cross1 + step1 * step1 * square1
    mix1 = norm2 / norm1
    sol_ref[...] = step0 * base[...] + step1 * direct[...]
    resid[...] = resid[...] - step1 * image_next[...]
    direct[...] = resid[...] + mix1 * direct[...]
    take_products(2, image_next, twice)
    image[...] = (resid_image[...] - step1 * twice[...]) + mix1 * image_next[...]
    sums_start(2, 0, pack(direct[...] * image[...]))
    sums_start(2, 1, sums_finish(2, 0))
    sums_start(2, 2, sums_finish(2, 1))
    total = sums_finish(2, 2)
    step2 = norm2 / scalar(total, 0)
    sol_ref[...] = sol_ref[...] + step2 * direct[...]
    res_ref[...] = resid[...] - step2 * image[...]

    for k in range(ITERS):
        drain_field(k)
        drain_products(k)
        sums_drain(k)


def solution(mesh):
    tiles, subs = mesh.shape["tile"], mesh.shape["sub"]
    side = math.isqrt(tiles // 2)

    def on_device(right_side, point_order, noise_var, block_pairs, pair_blocks, diag_blocks):
        rhs, points = right_side.shape
        slots, block = pair_blocks.shape[:2]
        blk_dev = diag_blocks.shape[0]
        cfg = (tiles, subs, side, blk_dev, block, slots, rhs)
        slots_all = 2 * subs + 2 * side
        vec = pltpu.VMEM((rhs, points), F32)
        dma = pltpu.SemaphoreType.DMA
        return pl.pallas_call(
            functools.partial(kernel, cfg),
            out_shape=(jax.ShapeDtypeStruct((rhs, points), F32),) * 2,
            in_specs=[pl.BlockSpec(memory_space=pl.ANY)] * 6,
            out_specs=(pl.BlockSpec(memory_space=pltpu.VMEM),) * 2,
            scratch_shapes=[
                vec,
                pltpu.VMEM((1, points), jnp.int32),
                pltpu.VMEM((1, points), F32),
                pltpu.SMEM((2, slots), jnp.int32),
                pltpu.VMEM((slots, block, block), BF16),
                pltpu.VMEM((blk_dev, block, block), BF16),
                vec,
                vec,
                vec,
                vec,
                vec,
                vec,
                vec,
                vec,
                pltpu.VMEM((ITERS, (subs + 1) * blk_dev, rhs, block), BF16),
                pltpu.VMEM((1 + 2 * slots, rhs, block), F32),
                pltpu.VMEM((ITERS, 4, blk_dev, rhs, block), BF16),
                pltpu.VMEM((ITERS, subs, blk_dev, rhs, block), BF16),
                pltpu.VMEM((ITERS, blk_dev, rhs, block), BF16),
                pltpu.VMEM((8, 128), jnp.int32),
                pltpu.SMEM((8, 128), jnp.int32),
                pltpu.VMEM((ITERS, slots_all, 3, rhs, 128), F32),
                dma((5,)),
                dma((PARTS,)),
                dma,
                dma((ITERS, 4)),
                dma((ITERS, subs, 2)),
                dma((ITERS, 2)),
                dma((ITERS, 2)),
                dma((ITERS, 2)),
                dma((ITERS, 3)),
                dma((ITERS, subs)),
                dma((ITERS,)),
                dma((ITERS,)),
                dma((ITERS, slots_all)),
                dma((ITERS, slots_all)),
            ],
            compiler_params=pltpu.CompilerParams(
                collective_id=0, has_side_effects=True, vmem_limit_bytes=40 << 20
            ),
            name="block_pair_solve",
        )(
            right_side,
            point_order,
            noise_var.reshape(1, -1),
            block_pairs.T,
            pair_blocks,
            diag_blocks,
        )

    both = ("tile", "sub")
    return jax.shard_map(
        on_device,
        mesh=mesh,
        in_specs=(
            P(None, both),
            P(both, None),
            P(both),
            P(both, None),
            P(both, None, None),
            P(both, None, None),
        ),
        out_specs=(P(None, both), P(None, both)),
        check_vma=False,
    )
```

time: 265 us -> 97.9 us (0.37)
  blocking collectives: 131 us -> 0 us
  Pallas kernels: 0 us -> 90 us
  matrix products: 47.9 us -> 0 us
  starting transfers between devices: 26.8 us -> 0 us
  local copies, waits for them, and re-layouts: 28.7 us -> 5.91 us
  waiting for transfers between devices: 17.6 us -> 0 us
  other arithmetic: 10.6 us -> 0 us
    psum x12 -> x0, blocking collectives: 92.5 us -> none  [one_axis_at_a_time(): array = lax.psum(array, axis)]
    pallas_call x0 -> x1, Pallas kernels: none -> 90 us  [on_device(): pl.pallas_call(functools.partial(kernel, cfg), out_shape=(jax.ShapeDtypeS...]
    dot_general x15 -> x0, matrix products: 47.9 us -> none  [the longest x3 24.1 us: on_device(): jnp.einsum('pij,rpj->rpi', pair_blocks, from_cols, preferred_element_type...]
    all_to_all x4 -> x0, blocking collectives: 38 us -> none  [the longest x2 19.9 us: sent_and_summed(): lax.all_to_all(split_up(array, dim, length), axis, 0, 0, tiled=True)]
    gather x8 -> x0, local copies, waits for them, and re-layouts: 22.4 us -> none  [the longest x2 17.8 us: on_device(): curve_rhs = jnp.take(right_side, point_order[0], axis=1)]
    ppermute x6 -> x0, starting transfers between devices: 17.9 us -> none  [from_behind(): return lax.ppermute(block, axis, route)]
    all_to_all x2 -> x0, waiting for transfers between devices: 10 us -> none  [the longest x1 7.5 us: sent_and_summed(): lax.all_to_all(split_up(array, dim, length), axis, 0, 0, tiled=True)]
    all_to_all x2 -> x0, starting transfers between devices: 8.82 us -> none  [the longest x1 5.42 us: copy_for_each(): return lax.all_to_all(copies, axis, split_axis=0, concat_axis=0, tiled=True)]
  transfers between devices with their start and end apart: 8 -> 0, of which waited for: 8 -> 0; matrix products, arithmetic and copies ran while one was open for 2% -> 0% of each run, Pallas kernels for 0% -> 0%
where the time goes in v1:
time: 97.9 us; the launch traced here: 96.5 us
  Pallas kernels  90 us (92%)
  local copies, waits for them, and re-layouts  5.91 us (6%)
    pallas_call x1, Pallas kernels, on_device(): pl.pallas_call(functools.partial(kernel, cfg), out_shape=(jax.ShapeDtypeS...  90 us
    unnamed x12, local copies, waits for them, and re-layouts  5.91 us

profile of v1, /device:TPU:0, one launch (start us, length us, event | category | flops | bytes accessed | tf_op | source)
XLA Modules:
  0.0 96.5 jit_solution(1590934044661604968)
XLA Ops:
  0.6 0.0 copy-start
  0.6 1.6 %copy-done = bf16[16,256,256]{2,1,0:T(8,128)(2,1)S(1)} copy-done((bf16[16,256,256]{2,1,0:T(8,128)(2,1)S(1)}, bf16[16,256,256]{2,1,0:T(8,128)(2,1)}, u32[]{:S(2)}) %copy-start) | copy-done | bytes 2097176
  2.2 0.0 copy-start.1
  2.2 0.9 copy-done.1
  3.1 0.0 copy-start.2
  3.1 0.7 copy-done.2
  3.8 0.0 copy-start.3
  3.8 0.7 copy-done.3
  4.6 0.0 copy-start.4
  4.6 0.7 copy-done.4
  5.2 90.0 %block_pair_solve.1 = (f32[8,4096]{1,0:T(8,128)S(1)}, f32[8,4096]{1,0:T(8,128)S(1)}) custom-call(f32[8,4096]{1,0:T(8,128)S(1)} %copy-done.1, s32[1,4096]{1,0:T(1,128)S(1)} %copy-done.2, f32[1,4096]{1,0:T(1,128)S(1)} %bitcast.2, s32[2,96]{1,0:T(2,128)S(1)} %bitcast.3, bf16[96,256,256]{2,1,0:T(8,128)(2,1)} %blocks_hbm.1, bf16[16,256,256]{2,1,0:T(8,128)(2,1)S(1)} %copy-done), custom_call_target="tpu_custom_call" | custom-call | tf_op jit(solution)/shard_map/block_pair_solve/pallas_call | solution.py:552
  95.2 0.7 copy.10
  95.9 0.7 copy.11
Async XLA Ops:
  0.6 1.6 %copy-start = (bf16[16,256,256]{2,1,0:T(8,128)(2,1)S(1)}, bf16[16,256,256]{2,1,0:T(8,128)(2,1)}, u32[]{:S(2)}) copy-start(bf16[16,256,256]{2,1,0:T(8,128)(2,1)} %diag_hbm.1) | copy-start | bytes 6291460
  2.2 0.9 copy-start.1
  3.1 0.7 copy-start.2
  3.8 0.7 copy-start.3
  4.6 0.7 copy-start.4

commit v2 on v1

v2 whole, which is shorter than its diff:
```python
import functools
import math

import jax
import jax.numpy as jnp
from jax import lax
from jax.experimental import pallas as pl
from jax.experimental.pallas import tpu as pltpu
from jax.sharding import PartitionSpec as P

ITERS = 3
UNROLL = 24
PARTS = 6
LANES = 128
F32 = jnp.float32
BF16 = jnp.bfloat16
MESH = pl.DeviceIdType.MESH


def scope(name):
    return jax.named_scope(name)


def kernel(
    cfg,
    right_hbm,
    order_hbm,
    noise_hbm,
    pairs_hbm,
    blocks_hbm,
    diag_hbm,
    sol_ref,
    res_ref,
    right,
    order,
    noise,
    pairs,
    blocks,
    diag,
    base,
    image,
    twice,
    resid,
    direct,
    image_next,
    resid_image,
    own_part,
    field,
    field_ahead,
    products,
    parts_out,
    parts_in,
    to_ahead,
    from_behind,
    table_vec,
    table,
    sums,
    in_sem,
    blocks_sem,
    table_sem,
    field_send,
    field_recv,
    ahead_send,
    ahead_recv,
    part_send,
    part_recv,
    behind_send,
    behind_recv,
    sums_send,
    sums_recv,
):
    tiles, subs, side, blk_dev, block, slots, rhs = cfg
    half = blk_dev // 2
    t = lax.axis_index("tile")
    s = lax.axis_index("sub")
    core = lax.rem(t, 2)
    above = lax.rem(s + 1, subs)
    below = lax.rem(s + subs - 1, subs)
    across = lax.rem(s + 2, subs)
    has_behind = t > 0
    has_ahead = t < tiles - 1

    loads = [
        pltpu.make_async_copy(right_hbm, right, in_sem.at[0]),
        pltpu.make_async_copy(order_hbm, order, in_sem.at[1]),
        pltpu.make_async_copy(pairs_hbm, pairs, in_sem.at[2]),
        pltpu.make_async_copy(noise_hbm, noise, in_sem.at[3]),
        pltpu.make_async_copy(diag_hbm, diag, in_sem.at[4]),
    ]
    step = slots // PARTS
    block_loads = [
        pltpu.make_async_copy(
            blocks_hbm.at[pl.ds(i * step, step)],
            blocks.at[pl.ds(i * step, step)],
            blocks_sem.at[i],
        )
        for i in range(PARTS)
    ]
    group = core * subs + s
    chip_x = lax.rem(t // 2, side)
    chip_y = t // (2 * side)

    def column_partner(index):
        return (t - core + index // subs, lax.rem(index, subs))

    def x_partner(index):
        return ((chip_y * side + index) * 2 + core, s)

    def y_partner(index):
        return ((index * side + chip_x) * 2 + core, s)

    stages = (
        (2 * subs, group, column_partner, 0),
        (side, chip_x, x_partner, 2 * subs),
        (side, chip_y, y_partner, 2 * subs + side),
    )

    barrier = pltpu.get_barrier_semaphore()
    greeted = 0
    for count, mine, partner, unused in stages:
        for j in range(1, count):
            pl.semaphore_signal(
                barrier, inc=1, device_id=partner(lax.rem(mine + j, count)), device_id_type=MESH
            )
            greeted += 1
    far_ahead = (core == 1) & has_ahead
    far_behind = (core == 0) & has_behind

    @pl.when(far_ahead)
    def _():
        pl.semaphore_signal(barrier, inc=1, device_id=(t + 1, s), device_id_type=MESH)

    @pl.when(far_behind)
    def _():
        pl.semaphore_signal(barrier, inc=1, device_id=(t - 1, s), device_id_type=MESH)

    for copy in loads[:2]:
        copy.start()
    for copy in block_loads[:1]:
        copy.start()
    for copy in loads[2:]:
        copy.start()
    for copy in block_loads[1:]:
        copy.start()

    chunks = right.shape[1] // LANES

    def permute(i, carry):
        at = pl.multiple_of(i * LANES, LANES)
        index = jnp.broadcast_to(order[:, pl.ds(at, LANES)], (rhs, LANES))
        low = lax.bitwise_and(index, LANES - 1)
        high = lax.shift_right_logical(index, 7)
        out = jnp.zeros((rhs, LANES), F32)
        for h in range(chunks):
            picked = jnp.take_along_axis(right[:, h * LANES : (h + 1) * LANES], low, axis=1)
            out = jnp.where(high == h, picked, out)
        base[:, pl.ds(at, LANES)] = out
        return carry

    def put_field(k, values, h):
        for b in range(h * half, (h + 1) * half):
            at = (b - h * half) * block
            field[k, s * blk_dev + b] = values[:, at : at + block].astype(BF16)

    def pieces(k):
        return 2 if k == 0 else 1

    def field_piece(k, row, h):
        length = blk_dev // pieces(k)
        return field.at[k, pl.ds(row * blk_dev + h * length, length)]

    targets = (across, above, below)
    sources = (across, below, above)

    def field_copy(k, row, h, n):
        return pltpu.make_async_remote_copy(
            src_ref=field_piece(k, row, h),
            dst_ref=field_piece(k, row, h),
            send_sem=field_send.at[k, n, h],
            recv_sem=field_recv.at[k, row, h],
            device_id=(t, targets[n]),
            device_id_type=MESH,
        )

    def ahead_copy(k, h):
        length = blk_dev // pieces(k)
        return pltpu.make_async_remote_copy(
            src_ref=field_piece(k, 0, h),
            dst_ref=field_ahead.at[k, pl.ds(h * length, length)],
            send_sem=ahead_send.at[k, h],
            recv_sem=ahead_recv.at[k, h],
            device_id=(t - 1, s),
            device_id_type=MESH,
        )

    def pass_back(k, row, h):
        @pl.when((row == 0) & has_behind)
        def _():
            ahead_copy(k, h).start()

    def start_field(k, h):
        for n in range(3):
            field_copy(k, s, h, n).start()
        pass_back(k, s, h)

    def finish_field(k):
        for h in range(pieces(k)):
            for n in (1, 2, 0):
                field_copy(k, sources[n], h, n).wait_recv()
                pass_back(k, sources[n], h)

    def finish_ahead(k):
        @pl.when(has_ahead)
        def _():
            for h in range(pieces(k)):
                ahead_copy(k, h).wait_recv()

        for b in range(blk_dev):
            field[k, subs * blk_dev + b] = field_ahead[k, b]

    def drain_field(k):
        for h in range(pieces(k)):
            for n in range(3):
                field_copy(k, s, h, n).wait_send()

        @pl.when(has_behind)
        def _():
            for h in range(pieces(k)):
                ahead_copy(k, h).wait_send()

    def sums_copy(k, stage, j, incoming):
        count, mine, partner, offset = stages[stage]
        other = lax.rem(mine + j, count)
        at = offset + (other if incoming else mine)
        return pltpu.make_async_remote_copy(
            src_ref=sums.at[k, at],
            dst_ref=sums.at[k, at],
            send_sem=sums_send.at[k, offset + j],
            recv_sem=sums_recv.at[k, at],
            device_id=partner(other),
            device_id_type=MESH,
        )

    def sums_start(k, stage, values):
        count, mine, partner, offset = stages[stage]
        sums[k, offset + mine] = values
        for j in range(1, count):
            sums_copy(k, stage, j, False).start()

    def sums_finish(k, stage):
        count, mine, partner, offset = stages[stage]
        for j in range(1, count):
            sums_copy(k, stage, j, True).wait_recv()
        total = sums[k, offset]
        for j in range(1, count):
            total = total + sums[k, offset + j]
        return total

    def sums_drain(k):
        for stage in range(3):
            for j in range(1, stages[stage][0]):
                sums_copy(k, stage, j, False).wait_send()

    def fold(values):
        parts = [values[:, i : i + LANES] for i in range(0, values.shape[1], LANES)]
        while len(parts) > 1:
            parts = [a + b for a, b in zip(parts[::2], parts[1::2])]
        return parts[0]

    spot = lax.broadcasted_iota(jnp.int32, (rhs, LANES), 1) - lax.broadcasted_iota(
        jnp.int32, (rhs, LANES), 0
    )

    def pack(*folded):
        out = jnp.zeros((rhs, LANES), F32)
        for n, values in enumerate(folded):
            column = jnp.sum(values, axis=1, keepdims=True)
            out = jnp.where(spot == n * rhs, column, out)
        return jnp.sum(out, axis=0, keepdims=True)

    def unpack(total, n):
        wide = jnp.broadcast_to(total, (rhs, LANES))
        return jnp.sum(jnp.where(spot == n * rhs, wide, 0.0), axis=1, keepdims=True)

    first = t * (subs * blk_dev)
    tile_blocks = subs * blk_dev

    def build_table():
        shape = (8, LANES)
        sub_id = lax.broadcasted_iota(jnp.int32, shape, 0)
        lane_id = lax.broadcasted_iota(jnp.int32, shape, 1)
        ids = sub_id * LANES + lane_id

        def add_slot(i, carry):
            found, listed, low, high = carry
            for u in range(8):
                p = i * 8 + u
                row = pairs[0, p]
                col = pairs[1, p]
                live = row >= 0
                reach = jnp.where(col - first >= tile_blocks, 1, 0)
                place = jnp.where(reach == 1, low, high)
                low = low + reach
                high = high - (1 - reach)
                apart = col - row
                kind = jnp.where(apart == 1, 0, apart - (blk_dev - 2))
                key_col = jnp.where(live, (col - first) * 8 + kind, -1)
                key_row = jnp.where(live, (row - first) * 8 + 4 + kind, -1)
                found = jnp.where(ids == key_col, place + 1, found)
                found = jnp.where(ids == key_row, place + 1 + slots, found)
                entry = jnp.where(
                    sub_id == 0,
                    p,
                    jnp.where(
                        sub_id == 1, jnp.maximum(row - first, 0), jnp.maximum(col - first, 0)
                    ),
                )
                listed = jnp.where(lane_id == place, entry, listed)
            return found, listed, low, high

        zeros = jnp.zeros(shape, jnp.int32)
        found, listed, unused_low, unused_high = lax.fori_loop(
            0, slots // 8, add_slot, (zeros, zeros, jnp.int32(0), jnp.int32(slots - 1))
        )
        table_vec[0:8] = found
        table_vec[8:16] = listed
        move = pltpu.make_async_copy(table_vec, table, table_sem)
        move.start()
        move.wait()
        products[0] = jnp.zeros((rhs, block), F32)

    def diag_products(k):
        def body(i, carry):
            for u in range(8):
                b = i * 8 + u
                at = pl.multiple_of(b * block, block)
                own_part[:, pl.ds(at, block)] = jnp.dot(
                    field[k, s * blk_dev + b], diag[b], preferred_element_type=F32
                )
            return carry

        lax.fori_loop(0, blk_dev // 8, body, 0)

    def col_products(k, low, high):
        def body(i, carry):
            for u in range(UNROLL):
                p = i * UNROLL + u
                products[1 + p] = lax.dot_general(
                    field[k, table[9, p]],
                    blocks[table[8, p]],
                    (((1,), (0,)), ((), ())),
                    preferred_element_type=F32,
                )
            return carry

        lax.fori_loop(low // UNROLL, high // UNROLL, body, 0)

    def row_products(k, low, high):
        def body(i, carry):
            for u in range(UNROLL):
                p = i * UNROLL + u
                products[1 + slots + p] = lax.dot_general(
                    field[k, table[10, p]],
                    blocks[table[8, p]],
                    (((1,), (1,)), ((), ())),
                    preferred_element_type=F32,
                )
            return carry

        lax.fori_loop(low // UNROLL, high // UNROLL, body, 0)

    def quadratic(k):
        def body(i, total):
            for u in range(8):
                p = i * 8 + u
                total = total + products[1 + p] * field[k, table[10, p]].astype(F32)
            return total

        return fold(lax.fori_loop(0, slots // 8, body, jnp.zeros((rhs, block), F32)))

    def gathered_sum(row, b, kinds):
        at = (row * blk_dev + b) * 8
        line = at // LANES
        lane = lax.rem(at, LANES)
        parts = [products[table[line, lane + n]] for n in kinds]
        while len(parts) > 1:
            pairs_of = [x + y for x, y in zip(parts[::2], parts[1::2])]
            parts = pairs_of + parts[len(pairs_of) * 2 :]
        return parts[0]

    def partial_sum(k, row, b):
        behind = jnp.where(row == 0, from_behind[k, b].astype(F32), 0.0)
        return gathered_sum(row, b, range(8)) + behind

    def remote(src, dst, send, recv, target):
        return pltpu.make_async_remote_copy(
            src_ref=src,
            dst_ref=dst,
            send_sem=send,
            recv_sem=recv,
            device_id=target,
            device_id_type=MESH,
        )

    def part_copy(k, n):
        return remote(
            parts_out.at[k, n], parts_in.at[k, n], part_send.at[k, n], part_recv.at[k, n], (t, targets[n])
        )

    def behind_copy(k):
        return remote(
            to_ahead.at[k],
            from_behind.at[k],
            behind_send.at[k],
            behind_recv.at[k],
            (t + 1, s),
        )

    def send_ahead(k):
        @pl.when(has_ahead)
        def _():
            def body(i, carry):
                for u in range(8):
                    b = i * 8 + u
                    to_ahead[k, b] = gathered_sum(subs, b, (1, 2, 3)).astype(BF16)
                return carry

            lax.fori_loop(0, blk_dev // 8, body, 0)
            behind_copy(k).start()

    def send_products(k):
        @pl.when(has_behind)
        def _():
            behind_copy(k).wait_recv()

        for n in range(3):

            def body(i, carry):
                for u in range(8):
                    b = i * 8 + u
                    parts_out[k, n, b] = partial_sum(k, targets[n], b).astype(BF16)
                return carry

            lax.fori_loop(0, blk_dev // 8, body, 0)
            part_copy(k, n).start()

    def own_products(k):
        def body(i, carry):
            for u in range(4):
                b = i * 4 + u
                at = pl.ds(pl.multiple_of(b * block, block), block)
                own_part[:, at] = own_part[:, at] + partial_sum(k, s, b)
            return carry

        lax.fori_loop(0, blk_dev // 4, body, 0)

    def take_products(k, vector, out):
        for n in (1, 2, 0):
            part_copy(k, n).wait_recv()
        for b in range(blk_dev):
            at = slice(b * block, (b + 1) * block)
            total = parts_in[k, 0, b].astype(F32) + parts_in[k, 1, b].astype(F32)
            total = total + parts_in[k, 2, b].astype(F32)
            out[:, at] = total + (own_part[:, at] + noise[:, at] * vector[:, at])

    def drain_products(k):
        for n in range(3):
            part_copy(k, n).wait_send()

        @pl.when(has_ahead)
        def _():
            behind_copy(k).wait_send()

    middle = slots // 2

    loads[0].wait()
    loads[1].wait()
    with scope("permute0"):
        lax.fori_loop(0, chunks // 2, permute, 0)
        put_field(0, base[:, 0 : half * block], 0)
    with scope("barrier"):
        pl.semaphore_wait(barrier, greeted + jnp.where(far_ahead | far_behind, 1, 0))
    start_field(0, 0)
    with scope("permute1"):
        lax.fori_loop(chunks // 2, chunks, permute, 0)
        put_field(0, base[:, half * block :], 1)
    start_field(0, 1)

    @pl.when(jnp.logical_not(has_ahead))
    def _():
        for k in range(ITERS):
            field_ahead[k] = jnp.zeros((blk_dev, rhs, block), BF16)

    @pl.when(jnp.logical_not(has_behind))
    def _():
        for k in range(ITERS):
            from_behind[k] = jnp.zeros((blk_dev, rhs, block), BF16)

    loads[2].wait()
    with scope("table"):
        build_table()
    loads[4].wait()
    with scope("diag0"):
        diag_products(0)
    with scope("finish0"):
        finish_field(0)
    for copy in block_loads:
        copy.wait()
    with scope("cols0"):
        col_products(0, 0, middle)
        send_ahead(0)
        col_products(0, middle, slots)
    with scope("rows0"):
        row_products(0, middle, slots)
        finish_ahead(0)
        row_products(0, 0, middle)
    with scope("send0"):
        send_products(0)
    with scope("own0"):
        own_products(0)
    loads[3].wait()
    with scope("take0"):
        take_products(0, base, image)

    with scope("start1"):
        put_field(1, image[:, 0 : half * block], 0)
        put_field(1, image[:, half * block :], 1)
        start_field(1, 0)
    with scope("sums0"):
        b_now = base[...]
        q_now = image[...]
        sums_start(0, 0, pack(fold(b_now * b_now), fold(b_now * q_now), fold(q_now * q_now)))
    with scope("diag1"):
        diag_products(1)
    with scope("finish1"):
        finish_field(1)
    with scope("sums0b"):
        sums_start(0, 1, sums_finish(0, 0))
    with scope("cols1"):
        col_products(1, 0, middle)
        send_ahead(1)
        col_products(1, middle, slots)
    with scope("sums0c"):
        sums_start(0, 2, sums_finish(0, 1))
    with scope("rows1"):
        row_products(1, middle, slots)
        finish_ahead(1)
        row_products(1, 0, middle)
    with scope("send1"):
        send_products(1)
    with scope("own1"):
        own_products(1)
    with scope("sums0d"):
        total = sums_finish(0, 2)
        norm0 = unpack(total, 0)
        curve0 = unpack(total, 1)
        square0 = unpack(total, 2)
        step0 = norm0 / curve0
        rate0 = curve0 / norm0
        norm1 = norm0 - 2.0 * step0 * curve0 + step0 * step0 * square0
        mix0 = norm1 / norm0
        resid[...] = base[...] - step0 * image[...]
        direct[...] = resid[...] + mix0 * base[...]
    with scope("take1"):
        take_products(1, image, twice)

    with scope("start2"):
        resid_image[...] = image[...] - step0 * twice[...]
        image_next[...] = resid_image[...] + mix0 * image[...]
        image[...] = image_next[...] - rate0 * resid[...]
        put_field(2, image[:, 0 : half * block], 0)
        put_field(2, image[:, half * block :], 1)
        start_field(2, 0)
    with scope("sums1"):
        q_now = image_next[...]
        sums_start(
            1,
            0,
            pack(
                fold(direct[...] * q_now),
                fold(resid[...] * q_now),
                fold(q_now * q_now),
                fold(resid[...] * resid_image[...]),
                fold(q_now * resid_image[...]),
            ),
        )
    with scope("diag2"):
        diag_products(2)
        w_now = image[...]
        local = fold(w_now * (own_part[...] + noise[...] * w_now))
    with scope("finish2"):
        finish_field(2)
    with scope("sums1b"):
        sums_start(1, 1, sums_finish(1, 0))
    with scope("cols2"):
        col_products(2, 0, middle)
        send_ahead(2)
        col_products(2, middle, slots)
        finish_ahead(2)
    with scope("sums2"):
        sums_start(2, 0, pack(local + 2.0 * quadratic(2)))
        sums_start(1, 2, sums_finish(1, 1))
    with scope("rows2"):
        row_products(2, 0, slots)
    with scope("sums2b"):
        sums_start(2, 1, sums_finish(2, 0))
    with scope("send2"):
        send_products(2)
    with scope("own2"):
        own_products(2)
    with scope("sums2c"):
        sums_start(2, 2, sums_finish(2, 1))
    with scope("sums2d"):
        total = sums_finish(1, 2)
        curve1 = unpack(total, 0)
        cross1 = unpack(total, 1)
        square1 = unpack(total, 2)
        inner_rr = unpack(total, 3)
        inner_qr = unpack(total, 4)
        step1 = norm1 / curve1
        norm2 = norm1 - 2.0 * step1 * cross1 + step1 * step1 * square1
        mix1 = norm2 / norm1
        keep = 1.0 - step1 * rate0
        inner_ww = unpack(sums_finish(2, 2), 0)
        inner_wr = inner_qr - rate0 * inner_rr
        inner_wq = square1 - rate0 * cross1
        curve2 = (
            step1 * step1 * inner_ww
            + keep * keep * inner_rr
            + mix1 * mix1 * curve1
            - 2.0 * keep * step1 * inner_wr
            + 2.0 * keep * mix1 * cross1
            - 2.0 * step1 * mix1 * inner_wq
        )
        step2 = norm2 / curve2
        r_now = resid[...] - step1 * image_next[...]
        d_now = r_now + mix1 * direct[...]
        sol_ref[...] = step0 * base[...] + step1 * direct[...] + step2 * d_now
        resid[...] = r_now - step2 * (keep * resid_image[...] + mix1 * image_next[...])
    with scope("take2"):
        take_products(2, image, twice)
        res_ref[...] = resid[...] + (step2 * step1) * twice[...]

    with scope("drain"):
        for k in range(ITERS):
            drain_field(k)
            drain_products(k)
            sums_drain(k)


def solution(mesh):
    tiles, subs = mesh.shape["tile"], mesh.shape["sub"]
    side = math.isqrt(tiles // 2)

    def on_device(right_side, point_order, noise_var, block_pairs, pair_blocks, diag_blocks):
        rhs, points = right_side.shape
        slots, block = pair_blocks.shape[:2]
        blk_dev = diag_blocks.shape[0]
        cfg = (tiles, subs, side, blk_dev, block, slots, rhs)
        members = 2 * subs + 2 * side
        vec = pltpu.VMEM((rhs, points), F32)
        row = pltpu.VMEM((ITERS, blk_dev, rhs, block), BF16)
        dma = pltpu.SemaphoreType.DMA
        return pl.pallas_call(
            functools.partial(kernel, cfg),
            out_shape=(jax.ShapeDtypeStruct((rhs, points), F32),) * 2,
            in_specs=[pl.BlockSpec(memory_space=pltpu.MemorySpace.HBM)] * 6,
            out_specs=(pl.BlockSpec(memory_space=pltpu.VMEM),) * 2,
            scratch_shapes=[
                vec,
                pltpu.VMEM((1, points), jnp.int32),
                pltpu.VMEM((1, points), F32),
                pltpu.SMEM((2, slots), jnp.int32),
                pltpu.VMEM((slots, block, block), BF16),
                pltpu.VMEM((blk_dev, block, block), BF16),
                vec,
                vec,
                vec,
                vec,
                vec,
                vec,
                vec,
                vec,
                pltpu.VMEM((ITERS, (subs + 1) * blk_dev, rhs, block), BF16),
                row,
                pltpu.VMEM((1 + 2 * slots, rhs, block), F32),
                pltpu.VMEM((ITERS, 3, blk_dev, rhs, block), BF16),
                pltpu.VMEM((ITERS, 3, blk_dev, rhs, block), BF16),
                row,
                row,
                pltpu.VMEM((16, LANES), jnp.int32),
                pltpu.SMEM((16, LANES), jnp.int32),
                pltpu.VMEM((ITERS, members, 1, LANES), F32),
                dma((5,)),
                dma((PARTS,)),
                dma,
                dma((ITERS, 3, 2)),
                dma((ITERS, subs, 2)),
                dma((ITERS, 2)),
                dma((ITERS, 2)),
                dma((ITERS, 3)),
                dma((ITERS, 3)),
                dma((ITERS,)),
                dma((ITERS,)),
                dma((ITERS, members)),
                dma((ITERS, members)),
            ],
            compiler_params=pltpu.CompilerParams(
                collective_id=0, has_side_effects=True, vmem_limit_bytes=67043328
            ),
            name="block_pair_solve",
        )(
            right_side,
            point_order,
            noise_var.reshape(1, -1),
            block_pairs.T,
            pair_blocks,
            diag_blocks,
        )

    both = ("tile", "sub")
    return jax.shard_map(
        on_device,
        mesh=mesh,
        in_specs=(
            P(None, both),
            P(both, None),
            P(both),
            P(both, None),
            P(both, None, None),
            P(both, None, None),
        ),
        out_specs=(P(None, both), P(None, both)),
        check_vma=False,
    )
```

time: 97.9 us -> 67.6 us (0.69); the launches traced: 96.5 us -> 67.5 us
  Pallas kernels: 90 us -> 63.7 us
  local copies, waits for them, and re-layouts: 5.91 us -> 3.14 us
    pallas_call x1, Pallas kernels: 90 us -> 63.7 us  [on_device(): pl.pallas_call(functools.partial(kernel, cfg), out_shape=(jax.ShapeDtypeS...]
    unnamed x12 -> x2, local copies, waits for them, and re-layouts: 5.91 us -> 3.14 us
where the time goes in v2:
time: 67.6 us; the launch traced here: 67.5 us
  Pallas kernels  63.7 us (94%)
  local copies, waits for them, and re-layouts  3.14 us (5%)
    pallas_call x1, Pallas kernels, on_device(): pl.pallas_call(functools.partial(kernel, cfg), out_shape=(jax.ShapeDtypeS...  63.7 us
    unnamed x2, local copies, waits for them, and re-layouts  3.14 us

profile of v2, /device:TPU:0, one launch (start us, length us, event | category | flops | bytes accessed | tf_op | source)
XLA Modules:
  0.0 67.5 jit_solution(11909877550759885108)
XLA Ops:
  0.6 63.7 %block_pair_solve.1 = (f32[8,4096]{1,0:T(8,128)}, f32[8,4096]{1,0:T(8,128)}) custom-call(f32[8,4096]{1,0:T(8,128)} %right_hbm.1, s32[1,4096]{1,0:T(1,128)} %order_hbm.1, f32[1,4096]{1,0:T(1,128)} %bitcast.2, s32[2,96]{1,0:T(2,128)} %bitcast.3, bf16[96,256,256]{2,1,0:T(8,128)(2,1)} %blocks_hbm.1, bf16[16,256,256]{2,1,0:T(8,128)(2,1)} %diag_hbm.1), custom_call_target="tpu_custom_call" | custom-call | tf_op jit(solution)/shard_map/block_pair_solve/pallas_call | solution.py:664
  64.3 1.6 %copy.10 = f32[8,4096]{1,0:T(8,128)} copy(f32[8,4096]{1,0:T(8,128)} %get-tuple-element.4) | data formatting | bytes 262144
  65.9 1.6 %copy.11 = f32[8,4096]{1,0:T(8,128)} copy(f32[8,4096]{1,0:T(8,128)} %get-tuple-element.5) | data formatting | bytes 262144

commit v3 on v2

--- a/solution.py
+++ b/solution.py
@@ -9,7 +9,6 @@
 from jax.sharding import PartitionSpec as P
 
 ITERS = 3
-UNROLL = 24
 PARTS = 6
 LANES = 128
 F32 = jnp.float32
@@ -47,7 +46,10 @@
     own_part,
     field,
     field_ahead,
-    products,
+    col_out,
+    row_out,
+    half_sums,
+    turned,
     parts_out,
     parts_in,
     to_ahead,
@@ -96,6 +98,9 @@
         )
         for i in range(PARTS)
     ]
+    for copy in loads[:2]:
+        copy.start()
+
     group = core * subs + s
     chip_x = lax.rem(t // 2, side)
     chip_y = t // (2 * side)
@@ -108,12 +113,19 @@
 
     def y_partner(index):
         return ((index * side + chip_x) * 2 + core, s)
+
+    def plane_partner(index):
+        return (index * 2 + core, s)
 
     stages = (
         (2 * subs, group, column_partner, 0),
         (side, chip_x, x_partner, 2 * subs),
         (side, chip_y, y_partner, 2 * subs + side),
     )
+    last_stages = (stages[0], (tiles // 2, t // 2, plane_partner, 2 * subs))
+
+    def stages_of(k):
+        return last_stages if k == ITERS - 1 else stages
 
     barrier = pltpu.get_barrier_semaphore()
     greeted = 0
@@ -134,8 +146,6 @@
     def _():
         pl.semaphore_signal(barrier, inc=1, device_id=(t - 1, s), device_id_type=MESH)
 
-    for copy in loads[:2]:
-        copy.start()
     for copy in block_loads[:1]:
         copy.start()
     for copy in loads[2:]:
@@ -229,7 +239,7 @@
                 ahead_copy(k, h).wait_send()
 
     def sums_copy(k, stage, j, incoming):
-        count, mine, partner, offset = stages[stage]
+        count, mine, partner, offset = stages_of(k)[stage]
         other = lax.rem(mine + j, count)
         at = offset + (other if incoming else mine)
         return pltpu.make_async_remote_copy(
@@ -242,13 +252,13 @@
         )
 
     def sums_start(k, stage, values):
-        count, mine, partner, offset = stages[stage]
+        count, mine, partner, offset = stages_of(k)[stage]
         sums[k, offset + mine] = values
         for j in range(1, count):
             sums_copy(k, stage, j, False).start()
 
     def sums_finish(k, stage):
-        count, mine, partner, offset = stages[stage]
+        count, mine, partner, offset = stages_of(k)[stage]
         for j in range(1, count):
             sums_copy(k, stage, j, True).wait_recv()
         total = sums[k, offset]
@@ -257,8 +267,8 @@
         return total
 
     def sums_drain(k):
-        for stage in range(3):
-            for j in range(1, stages[stage][0]):
+        for stage, (count, *unused) in enumerate(stages_of(k)):
+            for j in range(1, count):
                 sums_copy(k, stage, j, False).wait_send()
 
     def fold(values):
@@ -283,6 +293,7 @@
         return jnp.sum(jnp.where(spot == n * rhs, wide, 0.0), axis=1, keepdims=True)
 
     first = t * (subs * blk_dev)
+    middle = slots // 2
     tile_blocks = subs * blk_dev
 
     def build_table():
@@ -304,10 +315,9 @@
                 high = high - (1 - reach)
                 apart = col - row
                 kind = jnp.where(apart == 1, 0, apart - (blk_dev - 2))
-                key_col = jnp.where(live, (col - first) * 8 + kind, -1)
-                key_row = jnp.where(live, (row - first) * 8 + 4 + kind, -1)
-                found = jnp.where(ids == key_col, place + 1, found)
-                found = jnp.where(ids == key_row, place + 1 + slots, found)
+                key_col = jnp.where(live, (col - first) * 4 + kind, -1)
+                key_row = jnp.where(live, (row - first) * 4 + kind + 4 * LANES, -1)
+                found = jnp.where((ids == key_col) | (ids == key_row), place + 1, found)
                 entry = jnp.where(
                     sub_id == 0,
                     p,
@@ -327,7 +337,8 @@
         move = pltpu.make_async_copy(table_vec, table, table_sem)
         move.start()
         move.wait()
-        products[0] = jnp.zeros((rhs, block), F32)
+        col_out[0] = jnp.zeros((rhs, block), F32)
+        row_out[0] = jnp.zeros((rhs, block), F32)
 
     def diag_products(k):
         def body(i, carry):
@@ -341,56 +352,75 @@
 
         lax.fori_loop(0, blk_dev // 8, body, 0)
 
-    def col_products(k, low, high):
-        def body(i, carry):
-            for u in range(UNROLL):
-                p = i * UNROLL + u
-                products[1 + p] = lax.dot_general(
-                    field[k, table[9, p]],
-                    blocks[table[8, p]],
-                    (((1,), (0,)), ((), ())),
+    def listed_sum(out, line, q, kinds):
+        at = q * 4
+        row = line + at // LANES
+        lane = lax.rem(at, LANES)
+        parts = [out[table[row, lane + n]] for n in kinds]
+        while len(parts) > 1:
+            paired = [x + y for x, y in zip(parts[::2], parts[1::2])]
+            parts = paired + parts[len(paired) * 2 :]
+        return parts[0]
+
+    across_rows = (((1,), (0,)), ((), ()))
+    across_cols = (((1,), (1,)), ((), ()))
+
+    def turn(p):
+        turned[p] = blocks[table[8, p]].T
+
+    def col_products(k, low, also=()):
+        total = jnp.zeros((rhs, block), F32)
+        for u in range(middle):
+            p = low + u
+            out = lax.dot_general(
+                field[k, table[9, p]],
+                blocks[table[8, p]],
+                across_rows,
+                preferred_element_type=F32,
+            )
+            col_out[1 + p] = out
+            if k == ITERS - 1 and low > 0:
+                total = total + out * field[k, table[10, p]].astype(F32)
+            if u % 2 == 0 and u // 2 < len(also):
+                turn(also[u // 2])
+        return total
+
+    def row_products(k, low, is_turned, line, also=()):
+        share = tile_blocks // 2
+        for u in range(middle):
+            p = low + u
+            if is_turned(p):
+                row_out[1 + p] = lax.dot_general(
+                    field[k, table[10, p]],
+                    turned[p],
+                    across_rows,
                     preferred_element_type=F32,
                 )
-            return carry
-
-        lax.fori_loop(low // UNROLL, high // UNROLL, body, 0)
-
-    def row_products(k, low, high):
-        def body(i, carry):
-            for u in range(UNROLL):
-                p = i * UNROLL + u
-                products[1 + slots + p] = lax.dot_general(
+            else:
+                row_out[1 + p] = lax.dot_general(
                     field[k, table[10, p]],
                     blocks[table[8, p]],
-                    (((1,), (1,)), ((), ())),
+                    across_cols,
                     preferred_element_type=F32,
                 )
-            return carry
-
-        lax.fori_loop(low // UNROLL, high // UNROLL, body, 0)
-
-    def quadratic(k):
+            if u < share:
+                q = line * share + u
+                half_sums[q] = listed_sum(col_out, 0, q, range(4))
+            if u % 2 == 0 and u // 2 < len(also):
+                turn(also[u // 2])
+
+    def quadratic(k, total):
         def body(i, total):
             for u in range(8):
                 p = i * 8 + u
-                total = total + products[1 + p] * field[k, table[10, p]].astype(F32)
+                total = total + col_out[1 + p] * field[k, table[10, p]].astype(F32)
             return total
 
-        return fold(lax.fori_loop(0, slots // 8, body, jnp.zeros((rhs, block), F32)))
-
-    def gathered_sum(row, b, kinds):
-        at = (row * blk_dev + b) * 8
-        line = at // LANES
-        lane = lax.rem(at, LANES)
-        parts = [products[table[line, lane + n]] for n in kinds]
-        while len(parts) > 1:
-            pairs_of = [x + y for x, y in zip(parts[::2], parts[1::2])]
-            parts = pairs_of + parts[len(pairs_of) * 2 :]
-        return parts[0]
-
-    def partial_sum(k, row, b):
-        behind = jnp.where(row == 0, from_behind[k, b].astype(F32), 0.0)
-        return gathered_sum(row, b, range(8)) + behind
+        return fold(lax.fori_loop(0, middle // 8, body, total))
+
+    def partial_sum(row, b):
+        q = row * blk_dev + b
+        return half_sums[q] + listed_sum(row_out, 4, q, range(4))
 
     def remote(src, dst, send, recv, target):
         return pltpu.make_async_remote_copy(
@@ -422,7 +452,8 @@
             def body(i, carry):
                 for u in range(8):
                     b = i * 8 + u
-                    to_ahead[k, b] = gathered_sum(subs, b, (1, 2, 3)).astype(BF16)
+                    q = subs * blk_dev + b
+                    to_ahead[k, b] = listed_sum(col_out, 0, q, (1, 2, 3)).astype(BF16)
                 return carry
 
             lax.fori_loop(0, blk_dev // 8, body, 0)
@@ -433,12 +464,15 @@
         def _():
             behind_copy(k).wait_recv()
 
+        for b in range(blk_dev):
+            half_sums[b] = half_sums[b] + from_behind[k, b].astype(F32)
+
         for n in range(3):
 
             def body(i, carry):
                 for u in range(8):
                     b = i * 8 + u
-                    parts_out[k, n, b] = partial_sum(k, targets[n], b).astype(BF16)
+                    parts_out[k, n, b] = partial_sum(targets[n], b).astype(BF16)
                 return carry
 
             lax.fori_loop(0, blk_dev // 8, body, 0)
@@ -449,7 +483,7 @@
             for u in range(4):
                 b = i * 4 + u
                 at = pl.ds(pl.multiple_of(b * block, block), block)
-                own_part[:, at] = own_part[:, at] + partial_sum(k, s, b)
+                own_part[:, at] = own_part[:, at] + partial_sum(s, b)
             return carry
 
         lax.fori_loop(0, blk_dev // 4, body, 0)
@@ -471,7 +505,6 @@
         def _():
             behind_copy(k).wait_send()
 
-    middle = slots // 2
 
     loads[0].wait()
     loads[1].wait()
@@ -507,13 +540,14 @@
     for copy in block_loads:
         copy.wait()
     with scope("cols0"):
-        col_products(0, 0, middle)
+        quarter = middle // 2
+        col_products(0, 0, range(middle, middle + quarter))
         send_ahead(0)
-        col_products(0, middle, slots)
+        col_products(0, middle, range(middle + quarter, slots))
     with scope("rows0"):
-        row_products(0, middle, slots)
+        row_products(0, middle, lambda p: True, 0, range(quarter))
         finish_ahead(0)
-        row_products(0, 0, middle)
+        row_products(0, 0, lambda p: p < quarter, 1, range(quarter, middle))
     with scope("send0"):
         send_products(0)
     with scope("own0"):
@@ -522,14 +556,14 @@
     with scope("take0"):
         take_products(0, base, image)
 
+    with scope("sums0"):
+        b_now = base[...]
+        q_now = image[...]
+        sums_start(0, 0, pack(fold(b_now * b_now), fold(b_now * q_now), fold(q_now * q_now)))
     with scope("start1"):
         put_field(1, image[:, 0 : half * block], 0)
         put_field(1, image[:, half * block :], 1)
         start_field(1, 0)
-    with scope("sums0"):
-        b_now = base[...]
-        q_now = image[...]
-        sums_start(0, 0, pack(fold(b_now * b_now), fold(b_now * q_now), fold(q_now * q_now)))
     with scope("diag1"):
         diag_products(1)
     with scope("finish1"):
@@ -537,15 +571,16 @@
     with scope("sums0b"):
         sums_start(0, 1, sums_finish(0, 0))
     with scope("cols1"):
-        col_products(1, 0, middle)
+        col_products(1, 0)
         send_ahead(1)
-        col_products(1, middle, slots)
+        col_products(1, middle)
+    with scope("rows1"):
+        row_products(1, middle, lambda p: True, 0)
     with scope("sums0c"):
         sums_start(0, 2, sums_finish(0, 1))
-    with scope("rows1"):
-        row_products(1, middle, slots)
+    with scope("rows1b"):
         finish_ahead(1)
-        row_products(1, 0, middle)
+        row_products(1, 0, lambda p: True, 1)
     with scope("send1"):
         send_products(1)
     with scope("own1"):
@@ -568,9 +603,6 @@
         resid_image[...] = image[...] - step0 * twice[...]
         image_next[...] = resid_image[...] + mix0 * image[...]
         image[...] = image_next[...] - rate0 * resid[...]
-        put_field(2, image[:, 0 : half * block], 0)
-        put_field(2, image[:, half * block :], 1)
-        start_field(2, 0)
     with scope("sums1"):
         q_now = image_next[...]
         sums_start(
@@ -584,6 +616,10 @@
                 fold(q_now * resid_image[...]),
             ),
         )
+    with scope("start2b"):
+        put_field(2, image[:, 0 : half * block], 0)
+        put_field(2, image[:, half * block :], 1)
+        start_field(2, 0)
     with scope("diag2"):
         diag_products(2)
         w_now = image[...]
@@ -593,23 +629,24 @@
     with scope("sums1b"):
         sums_start(1, 1, sums_finish(1, 0))
     with scope("cols2"):
-        col_products(2, 0, middle)
+        col_products(2, 0)
         send_ahead(2)
-        col_products(2, middle, slots)
+        total = col_products(2, middle)
         finish_ahead(2)
     with scope("sums2"):
-        sums_start(2, 0, pack(local + 2.0 * quadratic(2)))
+        sums_start(2, 0, pack(local + 2.0 * quadratic(2, total)))
+    with scope("rows2"):
+        row_products(2, 0, lambda p: True, 0)
+    with scope("sums1c"):
         sums_start(1, 2, sums_finish(1, 1))
-    with scope("rows2"):
-        row_products(2, 0, slots)
+    with scope("rows2b"):
+        row_products(2, middle, lambda p: True, 1)
     with scope("sums2b"):
         sums_start(2, 1, sums_finish(2, 0))
     with scope("send2"):
         send_products(2)
     with scope("own2"):
         own_products(2)
-    with scope("sums2c"):
-        sums_start(2, 2, sums_finish(2, 1))
     with scope("sums2d"):
         total = sums_finish(1, 2)
         curve1 = unpack(total, 0)
@@ -621,7 +658,7 @@
         norm2 = norm1 - 2.0 * step1 * cross1 + step1 * step1 * square1
         mix1 = norm2 / norm1
         keep = 1.0 - step1 * rate0
-        inner_ww = unpack(sums_finish(2, 2), 0)
+        inner_ww = unpack(sums_finish(2, 1), 0)
         inner_wr = inner_qr - rate0 * inner_rr
         inner_wq = square1 - rate0 * cross1
         curve2 = (
@@ -657,7 +694,7 @@
         slots, block = pair_blocks.shape[:2]
         blk_dev = diag_blocks.shape[0]
         cfg = (tiles, subs, side, blk_dev, block, slots, rhs)
-        members = 2 * subs + 2 * side
+        members = 2 * subs + max(2 * side, tiles // 2)
         vec = pltpu.VMEM((rhs, points), F32)
         row = pltpu.VMEM((ITERS, blk_dev, rhs, block), BF16)
         dma = pltpu.SemaphoreType.DMA
@@ -683,7 +720,10 @@
                 vec,
                 pltpu.VMEM((ITERS, (subs + 1) * blk_dev, rhs, block), BF16),
                 row,
-                pltpu.VMEM((1 + 2 * slots, rhs, block), F32),
+                pltpu.VMEM((1 + slots, rhs, block), F32),
+                pltpu.VMEM((1 + slots, rhs, block), F32),
+                pltpu.VMEM((subs * blk_dev, rhs, block), F32),
+                pltpu.VMEM((slots, block, block), BF16),
                 pltpu.VMEM((ITERS, 3, blk_dev, rhs, block), BF16),
                 pltpu.VMEM((ITERS, 3, blk_dev, rhs, block), BF16),
                 row,
@@ -706,16 +746,21 @@
                 dma((ITERS, members)),
             ],
             compiler_params=pltpu.CompilerParams(
-                collective_id=0, has_side_effects=True, vmem_limit_bytes=67043328
+                collective_id=0, has_side_effects=True, vmem_limit_bytes=50 << 20
             ),
             name="block_pair_solve",
         )(
-            right_side,
-            point_order,
-            noise_var.reshape(1, -1),
-            block_pairs.T,
-            pair_blocks,
-            diag_blocks,
+            *(
+                pltpu.with_memory_space_constraint(value, pltpu.MemorySpace.HBM)
+                for value in (
+                    right_side,
+                    point_order,
+                    noise_var.reshape(1, -1),
+                    block_pairs.T,
+                    pair_blocks,
+                    diag_blocks,
+                )
+            )
         )
 
     both = ("tile", "sub")

time: 67.6 us -> 57.9 us (0.86)
  Pallas kernels: 63.7 us -> 55.8 us
  local copies, waits for them, and re-layouts: 3.14 us -> 1.31 us
    pallas_call x1, Pallas kernels: 63.7 us -> 55.8 us  [on_device(): pl.pallas_call(functools.partial(kernel, cfg), out_shape=(jax.ShapeDtypeS...]
    unnamed x2, local copies, waits for them, and re-layouts: 3.14 us -> 1.31 us
where the time goes in v3:
time: 57.9 us; the launch traced here: 57.8 us
  Pallas kernels  55.8 us (96%)
  local copies, waits for them, and re-layouts  1.31 us (2%)
  between operations  0.64 us (1%)
    pallas_call x1, Pallas kernels, on_device(): pl.pallas_call(functools.partial(kernel, cfg), out_shape=(jax.ShapeDtypeS...  55.8 us
    unnamed x2, local copies, waits for them, and re-layouts  1.31 us

profile of v3, /device:TPU:0, one launch (start us, length us, event | category | flops | bytes accessed | tf_op | source)
XLA Modules:
  0.0 57.8 jit_solution(9983470395311230757)
XLA Ops:
  0.6 55.8 %block_pair_solve.1 = (f32[8,4096]{1,0:T(8,128)S(1)}, f32[8,4096]{1,0:T(8,128)S(1)}) custom-call(f32[8,4096]{1,0:T(8,128)} %right_hbm.1, s32[1,4096]{1,0:T(1,128)} %order_hbm.1, f32[1,4096]{1,0:T(1,128)} %bitcast.2, s32[2,96]{1,0:T(2,128)} %bitcast.3, bf16[96,256,256]{2,1,0:T(8,128)(2,1)} %blocks_hbm.1, bf16[16,256,256]{2,1,0:T(8,128)(2,1)} %diag_hbm.1), custom_call_target="tpu_custom_call" | custom-call | tf_op jit(solution)/shard_map/block_pair_solve/pallas_call | solution.py:701
  56.5 0.7 %copy.10 = f32[8,4096]{1,0:T(8,128)} copy(f32[8,4096]{1,0:T(8,128)S(1)} %get-tuple-element.4) | data formatting | bytes 262144
  57.1 0.7 %copy.11 = f32[8,4096]{1,0:T(8,128)} copy(f32[8,4096]{1,0:T(8,128)S(1)} %get-tuple-element.5) | data formatting | bytes 262144

commit v4 on v3

--- a/solution.py
+++ b/solution.py
@@ -72,7 +72,6 @@
     sums_recv,
 ):
     tiles, subs, side, blk_dev, block, slots, rhs = cfg
-    half = blk_dev // 2
     t = lax.axis_index("tile")
     s = lax.axis_index("sub")
     core = lax.rem(t, 2)
@@ -94,7 +93,7 @@
         pltpu.make_async_copy(
             blocks_hbm.at[pl.ds(i * step, step)],
             blocks.at[pl.ds(i * step, step)],
-            blocks_sem.at[i],
+            blocks_sem,
         )
         for i in range(PARTS)
     ]
@@ -142,9 +141,18 @@
     def _():
         pl.semaphore_signal(barrier, inc=1, device_id=(t + 1, s), device_id_type=MESH)
 
+        @pl.when(s > 0)
+        def _():
+            pl.semaphore_signal(barrier, inc=1, device_id=(t + 1, 0), device_id_type=MESH)
+
     @pl.when(far_behind)
     def _():
         pl.semaphore_signal(barrier, inc=1, device_id=(t - 1, s), device_id_type=MESH)
+
+        @pl.when(s == 0)
+        def _():
+            for j in range(1, subs):
+                pl.semaphore_signal(barrier, inc=1, device_id=(t - 1, j), device_id_type=MESH)
 
     for copy in block_loads[:1]:
         copy.start()
@@ -156,57 +164,68 @@
     chunks = right.shape[1] // LANES
 
     def permute(i, carry):
-        at = pl.multiple_of(i * LANES, LANES)
-        index = jnp.broadcast_to(order[:, pl.ds(at, LANES)], (rhs, LANES))
-        low = lax.bitwise_and(index, LANES - 1)
-        high = lax.shift_right_logical(index, 7)
-        out = jnp.zeros((rhs, LANES), F32)
-        for h in range(chunks):
-            picked = jnp.take_along_axis(right[:, h * LANES : (h + 1) * LANES], low, axis=1)
-            out = jnp.where(high == h, picked, out)
-        base[:, pl.ds(at, LANES)] = out
+        for u in range(4):
+            chunk = (i % (chunks // 8) * 4 + u) * 2 + i // (chunks // 8)
+            at = pl.multiple_of(chunk * LANES, LANES)
+            index = jnp.broadcast_to(order[:, pl.ds(at, LANES)], (rhs, LANES))
+            low = lax.bitwise_and(index, LANES - 1)
+            high = lax.shift_right_logical(index, 7)
+            out = jnp.zeros((rhs, LANES), F32)
+            for h in range(chunks):
+                picked = jnp.take_along_axis(right[:, h * LANES : (h + 1) * LANES], low, axis=1)
+                out = jnp.where(high == h, picked, out)
+            base[:, pl.ds(at, LANES)] = out
         return carry
 
     def put_field(k, values, h):
-        for b in range(h * half, (h + 1) * half):
-            at = (b - h * half) * block
-            field[k, s * blk_dev + b] = values[:, at : at + block].astype(BF16)
-
-    def pieces(k):
-        return 2 if k == 0 else 1
-
-    def field_piece(k, row, h):
-        length = blk_dev // pieces(k)
-        return field.at[k, pl.ds(row * blk_dev + h * length, length)]
+        for b in range(blk_dev):
+            at = b * block + h * LANES
+            field[k, h, s * blk_dev + b] = values[:, at : at + LANES].astype(BF16)
+
+    def whole(k, q):
+        return jnp.concatenate([field[k, 0, q], field[k, 1, q]], axis=1)
+
+    def remote(src, dst, send, recv, target):
+        return pltpu.make_async_remote_copy(
+            src_ref=src,
+            dst_ref=dst,
+            send_sem=send,
+            recv_sem=recv,
+            device_id=target,
+            device_id_type=MESH,
+        )
 
     targets = (across, above, below)
     sources = (across, below, above)
 
     def field_copy(k, row, h, n):
-        return pltpu.make_async_remote_copy(
-            src_ref=field_piece(k, row, h),
-            dst_ref=field_piece(k, row, h),
-            send_sem=field_send.at[k, n, h],
-            recv_sem=field_recv.at[k, row, h],
-            device_id=(t, targets[n]),
-            device_id_type=MESH,
-        )
-
-    def ahead_copy(k, h):
-        length = blk_dev // pieces(k)
-        return pltpu.make_async_remote_copy(
-            src_ref=field_piece(k, 0, h),
-            dst_ref=field_ahead.at[k, pl.ds(h * length, length)],
-            send_sem=ahead_send.at[k, h],
-            recv_sem=ahead_recv.at[k, h],
-            device_id=(t - 1, s),
-            device_id_type=MESH,
-        )
+        part = field.at[k, h, pl.ds(row * blk_dev, blk_dev)]
+        return remote(part, part, field_send.at[k], field_recv.at[k, h, n], (t, targets[n]))
+
+    def ahead_copy(k, h, to):
+        return remote(
+            field.at[k, h, pl.ds(0, blk_dev)],
+            field_ahead.at[k, h],
+            ahead_send.at[k],
+            ahead_recv.at[k],
+            (t - 1, to),
+        )
+
+    def ahead_waits(k):
+        both = field_ahead.at[k]
+        return remote(both, both, ahead_send.at[k], ahead_recv.at[k], (t, above))
 
     def pass_back(k, row, h):
-        @pl.when((row == 0) & has_behind)
-        def _():
-            ahead_copy(k, h).start()
+        @pl.when((row == 0) & (core == 1))
+        def _():
+            ahead_copy(k, h, s).start()
+
+    def send_behind(k):
+        @pl.when((s == 0) & far_behind)
+        def _():
+            for h in range(2):
+                for j in (2, 1, 3, 0):
+                    ahead_copy(k, h, j).start()
 
     def start_field(k, h):
         for n in range(3):
@@ -214,62 +233,64 @@
         pass_back(k, s, h)
 
     def finish_field(k):
-        for h in range(pieces(k)):
-            for n in (1, 2, 0):
+        for n in (1, 2, 0):
+            for h in range(2):
                 field_copy(k, sources[n], h, n).wait_recv()
                 pass_back(k, sources[n], h)
 
     def finish_ahead(k):
         @pl.when(has_ahead)
         def _():
-            for h in range(pieces(k)):
-                ahead_copy(k, h).wait_recv()
-
-        for b in range(blk_dev):
-            field[k, subs * blk_dev + b] = field_ahead[k, b]
+            ahead_waits(k).wait_recv()
+
+        for h in range(2):
+            for b in range(blk_dev):
+                field[k, h, subs * blk_dev + b] = field_ahead[k, h, b]
 
     def drain_field(k):
-        for h in range(pieces(k)):
-            for n in range(3):
-                field_copy(k, s, h, n).wait_send()
-
-        @pl.when(has_behind)
-        def _():
-            for h in range(pieces(k)):
-                ahead_copy(k, h).wait_send()
-
-    def sums_copy(k, stage, j, incoming):
-        count, mine, partner, offset = stages_of(k)[stage]
-        other = lax.rem(mine + j, count)
-        at = offset + (other if incoming else mine)
-        return pltpu.make_async_remote_copy(
-            src_ref=sums.at[k, at],
-            dst_ref=sums.at[k, at],
-            send_sem=sums_send.at[k, offset + j],
-            recv_sem=sums_recv.at[k, at],
-            device_id=partner(other),
-            device_id_type=MESH,
-        )
+        sent = parts_out.at[k]
+        remote(sent, sent, field_send.at[k], field_recv.at[k, 0, 0], (t, above)).wait_send()
+
+        @pl.when(core == 1)
+        def _():
+            ahead_waits(k).wait_send()
+
+        @pl.when((s == 0) & far_behind)
+        def _():
+            sent = field.at[k, :, pl.ds(0, subs * blk_dev)]
+            remote(sent, sent, ahead_send.at[k], ahead_recv.at[k], (t, above)).wait_send()
 
     def sums_start(k, stage, values):
         count, mine, partner, offset = stages_of(k)[stage]
         sums[k, offset + mine] = values
+        own = sums.at[k, offset + mine]
         for j in range(1, count):
-            sums_copy(k, stage, j, False).start()
+            remote(
+                own,
+                own,
+                sums_send.at[k, stage],
+                sums_recv.at[k, stage],
+                partner(lax.rem(mine + j, count)),
+            ).start()
+
+    def sums_waits(k, stage):
+        count, mine, partner, offset = stages_of(k)[stage]
+        others = sums.at[k, pl.ds(offset, count - 1)]
+        return remote(
+            others, others, sums_send.at[k, stage], sums_recv.at[k, stage], (t, above)
+        )
 
     def sums_finish(k, stage):
         count, mine, partner, offset = stages_of(k)[stage]
-        for j in range(1, count):
-            sums_copy(k, stage, j, True).wait_recv()
+        sums_waits(k, stage).wait_recv()
         total = sums[k, offset]
         for j in range(1, count):
             total = total + sums[k, offset + j]
         return total
 
     def sums_drain(k):
-        for stage, (count, *unused) in enumerate(stages_of(k)):
-            for j in range(1, count):
-                sums_copy(k, stage, j, False).wait_send()
+        for stage in range(len(stages_of(k))):
+            sums_waits(k, stage).wait_send()
 
     def fold(values):
         parts = [values[:, i : i + LANES] for i in range(0, values.shape[1], LANES)]
@@ -346,7 +367,7 @@
                 b = i * 8 + u
                 at = pl.multiple_of(b * block, block)
                 own_part[:, pl.ds(at, block)] = jnp.dot(
-                    field[k, s * blk_dev + b], diag[b], preferred_element_type=F32
+                    whole(k, s * blk_dev + b), diag[b], preferred_element_type=F32
                 )
             return carry
 
@@ -368,19 +389,17 @@
     def turn(p):
         turned[p] = blocks[table[8, p]].T
 
+    def dot(left, right_block, dims):
+        return lax.dot_general(left, right_block, dims, preferred_element_type=F32)
+
     def col_products(k, low, also=()):
         total = jnp.zeros((rhs, block), F32)
         for u in range(middle):
             p = low + u
-            out = lax.dot_general(
-                field[k, table[9, p]],
-                blocks[table[8, p]],
-                across_rows,
-                preferred_element_type=F32,
-            )
+            out = dot(whole(k, table[9, p]), blocks[table[8, p]], across_rows)
             col_out[1 + p] = out
             if k == ITERS - 1 and low > 0:
-                total = total + out * field[k, table[10, p]].astype(F32)
+                total = total + out * whole(k, table[10, p]).astype(F32)
             if u % 2 == 0 and u // 2 < len(also):
                 turn(also[u // 2])
         return total
@@ -389,20 +408,11 @@
         share = tile_blocks // 2
         for u in range(middle):
             p = low + u
+            left = whole(k, table[10, p])
             if is_turned(p):
-                row_out[1 + p] = lax.dot_general(
-                    field[k, table[10, p]],
-                    turned[p],
-                    across_rows,
-                    preferred_element_type=F32,
-                )
+                row_out[1 + p] = dot(left, turned[p], across_rows)
             else:
-                row_out[1 + p] = lax.dot_general(
-                    field[k, table[10, p]],
-                    blocks[table[8, p]],
-                    across_cols,
-                    preferred_element_type=F32,
-                )
+                row_out[1 + p] = dot(left, blocks[table[8, p]], across_cols)
             if u < share:
                 q = line * share + u
                 half_sums[q] = listed_sum(col_out, 0, q, range(4))
@@ -413,7 +423,7 @@
         def body(i, total):
             for u in range(8):
                 p = i * 8 + u
-                total = total + col_out[1 + p] * field[k, table[10, p]].astype(F32)
+                total = total + col_out[1 + p] * whole(k, table[10, p]).astype(F32)
             return total
 
         return fold(lax.fori_loop(0, middle // 8, body, total))
@@ -422,19 +432,14 @@
         q = row * blk_dev + b
         return half_sums[q] + listed_sum(row_out, 4, q, range(4))
 
-    def remote(src, dst, send, recv, target):
-        return pltpu.make_async_remote_copy(
-            src_ref=src,
-            dst_ref=dst,
-            send_sem=send,
-            recv_sem=recv,
-            device_id=target,
-            device_id_type=MESH,
-        )
-
     def part_copy(k, n):
         return remote(
-            parts_out.at[k, n], parts_in.at[k, n], part_send.at[k, n], part_recv.at[k, n], (t, targets[n])
+            parts_out.at[k, n], parts_in.at[k, n], part_send.at[k], part_recv.at[k], (t, targets[n])
+        )
+
+    def part_waits(k):
+        return remote(
+            parts_out.at[k], parts_in.at[k], part_send.at[k], part_recv.at[k], (t, above)
         )
 
     def behind_copy(k):
@@ -489,8 +494,7 @@
         lax.fori_loop(0, blk_dev // 4, body, 0)
 
     def take_products(k, vector, out):
-        for n in (1, 2, 0):
-            part_copy(k, n).wait_recv()
+        part_waits(k).wait_recv()
         for b in range(blk_dev):
             at = slice(b * block, (b + 1) * block)
             total = parts_in[k, 0, b].astype(F32) + parts_in[k, 1, b].astype(F32)
@@ -498,8 +502,7 @@
             out[:, at] = total + (own_part[:, at] + noise[:, at] * vector[:, at])
 
     def drain_products(k):
-        for n in range(3):
-            part_copy(k, n).wait_send()
+        part_waits(k).wait_send()
 
         @pl.when(has_ahead)
         def _():
@@ -509,20 +512,24 @@
     loads[0].wait()
     loads[1].wait()
     with scope("permute0"):
-        lax.fori_loop(0, chunks // 2, permute, 0)
-        put_field(0, base[:, 0 : half * block], 0)
+        lax.fori_loop(0, chunks // 8, permute, 0)
+        put_field(0, base[...], 0)
     with scope("barrier"):
-        pl.semaphore_wait(barrier, greeted + jnp.where(far_ahead | far_behind, 1, 0))
+        pl.semaphore_wait(barrier, greeted
+            + jnp.where(far_ahead | far_behind, 1, 0)
+            + jnp.where(far_ahead & (s > 0), 1, 0)
+            + jnp.where(far_behind & (s == 0), subs - 1, 0))
     start_field(0, 0)
     with scope("permute1"):
-        lax.fori_loop(chunks // 2, chunks, permute, 0)
-        put_field(0, base[:, half * block :], 1)
+        lax.fori_loop(chunks // 8, chunks // 4, permute, 0)
+        put_field(0, base[...], 1)
     start_field(0, 1)
+    send_behind(0)
 
     @pl.when(jnp.logical_not(has_ahead))
     def _():
         for k in range(ITERS):
-            field_ahead[k] = jnp.zeros((blk_dev, rhs, block), BF16)
+            field_ahead[k] = jnp.zeros((2, blk_dev, rhs, LANES), BF16)
 
     @pl.when(jnp.logical_not(has_behind))
     def _():
@@ -535,10 +542,9 @@
     loads[4].wait()
     with scope("diag0"):
         diag_products(0)
+    pltpu.make_async_copy(blocks_hbm, blocks, blocks_sem).wait()
     with scope("finish0"):
         finish_field(0)
-    for copy in block_loads:
-        copy.wait()
     with scope("cols0"):
         quarter = middle // 2
         col_products(0, 0, range(middle, middle + quarter))
@@ -561,9 +567,11 @@
         q_now = image[...]
         sums_start(0, 0, pack(fold(b_now * b_now), fold(b_now * q_now), fold(q_now * q_now)))
     with scope("start1"):
-        put_field(1, image[:, 0 : half * block], 0)
-        put_field(1, image[:, half * block :], 1)
+        put_field(1, image[...], 0)
         start_field(1, 0)
+        put_field(1, image[...], 1)
+        start_field(1, 1)
+        send_behind(1)
     with scope("diag1"):
         diag_products(1)
     with scope("finish1"):
@@ -576,13 +584,13 @@
         col_products(1, middle)
     with scope("rows1"):
         row_products(1, middle, lambda p: True, 0)
-    with scope("sums0c"):
-        sums_start(0, 2, sums_finish(0, 1))
     with scope("rows1b"):
         finish_ahead(1)
         row_products(1, 0, lambda p: True, 1)
     with scope("send1"):
         send_products(1)
+    with scope("sums0c"):
+        sums_start(0, 2, sums_finish(0, 1))
     with scope("own1"):
         own_products(1)
     with scope("sums0d"):
@@ -617,9 +625,11 @@
             ),
         )
     with scope("start2b"):
-        put_field(2, image[:, 0 : half * block], 0)
-        put_field(2, image[:, half * block :], 1)
+        put_field(2, image[...], 0)
         start_field(2, 0)
+        put_field(2, image[...], 1)
+        start_field(2, 1)
+        send_behind(2)
     with scope("diag2"):
         diag_products(2)
         w_now = image[...]
@@ -636,15 +646,15 @@
     with scope("sums2"):
         sums_start(2, 0, pack(local + 2.0 * quadratic(2, total)))
     with scope("rows2"):
-        row_products(2, 0, lambda p: True, 0)
+        row_products(2, middle, lambda p: True, 0)
+    with scope("rows2b"):
+        row_products(2, 0, lambda p: True, 1)
+    with scope("send2"):
+        send_products(2)
+    with scope("sums2b"):
+        sums_start(2, 1, sums_finish(2, 0))
     with scope("sums1c"):
         sums_start(1, 2, sums_finish(1, 1))
-    with scope("rows2b"):
-        row_products(2, middle, lambda p: True, 1)
-    with scope("sums2b"):
-        sums_start(2, 1, sums_finish(2, 0))
-    with scope("send2"):
-        send_products(2)
     with scope("own2"):
         own_products(2)
     with scope("sums2d"):
@@ -718,8 +728,8 @@
                 vec,
                 vec,
                 vec,
-                pltpu.VMEM((ITERS, (subs + 1) * blk_dev, rhs, block), BF16),
-                row,
+                pltpu.VMEM((ITERS, 2, (subs + 1) * blk_dev, rhs, LANES), BF16),
+                pltpu.VMEM((ITERS, 2, blk_dev, rhs, LANES), BF16),
                 pltpu.VMEM((1 + slots, rhs, block), F32),
                 pltpu.VMEM((1 + slots, rhs, block), F32),
                 pltpu.VMEM((subs * blk_dev, rhs, block), F32),
@@ -732,18 +742,18 @@
                 pltpu.SMEM((16, LANES), jnp.int32),
                 pltpu.VMEM((ITERS, members, 1, LANES), F32),
                 dma((5,)),
-                dma((PARTS,)),
                 dma,
-                dma((ITERS, 3, 2)),
-                dma((ITERS, subs, 2)),
-                dma((ITERS, 2)),
-                dma((ITERS, 2)),
+                dma,
+                dma((ITERS,)),
+                dma((ITERS, 2, 3)),
+                dma((ITERS,)),
+                dma((ITERS,)),
+                dma((ITERS,)),
+                dma((ITERS,)),
+                dma((ITERS,)),
+                dma((ITERS,)),
                 dma((ITERS, 3)),
                 dma((ITERS, 3)),
-                dma((ITERS,)),
-                dma((ITERS,)),
-                dma((ITERS, members)),
-                dma((ITERS, members)),
             ],
             compiler_params=pltpu.CompilerParams(
                 collective_id=0, has_side_effects=True, vmem_limit_bytes=50 << 20

time: 57.9 us -> 54.8 us (0.946)
  Pallas kernels: 55.8 us -> 52.9 us
    pallas_call x1, Pallas kernels: 55.8 us -> 52.9 us  [on_device(): pl.pallas_call(functools.partial(kernel, cfg), out_shape=(jax.ShapeDtypeS...]
where the time goes in v4:
time: 54.8 us; the launch traced here: 54.9 us
  Pallas kernels  52.9 us (97%)
  local copies, waits for them, and re-layouts  1.31 us (2%)
  between operations  0.64 us (1%)
    pallas_call x1, Pallas kernels, on_device(): pl.pallas_call(functools.partial(kernel, cfg), out_shape=(jax.ShapeDtypeS...  52.9 us
    unnamed x2, local copies, waits for them, and re-layouts  1.31 us

profile of v4, /device:TPU:0, one launch (start us, length us, event | category | flops | bytes accessed | tf_op | source)
XLA Modules:
  0.0 54.9 jit_solution(17266375915955217168)
XLA Ops:
  0.6 52.9 %block_pair_solve.1 = (f32[8,4096]{1,0:T(8,128)S(1)}, f32[8,4096]{1,0:T(8,128)S(1)}) custom-call(f32[8,4096]{1,0:T(8,128)} %right_hbm.1, s32[1,4096]{1,0:T(1,128)} %order_hbm.1, f32[1,4096]{1,0:T(1,128)} %bitcast.2, s32[2,96]{1,0:T(2,128)} %bitcast.3, bf16[96,256,256]{2,1,0:T(8,128)(2,1)} %blocks_hbm.1, bf16[16,256,256]{2,1,0:T(8,128)(2,1)} %diag_hbm.1), custom_call_target="tpu_custom_call" | custom-call | tf_op jit(solution)/shard_map/block_pair_solve/pallas_call | solution.py:711
  53.6 0.7 %copy.10 = f32[8,4096]{1,0:T(8,128)} copy(f32[8,4096]{1,0:T(8,128)S(1)} %get-tuple-element.4) | data formatting | bytes 262144
  54.2 0.7 %copy.11 = f32[8,4096]{1,0:T(8,128)} copy(f32[8,4096]{1,0:T(8,128)S(1)} %get-tuple-element.5) | data formatting | bytes 262144

commit v5 on v4

--- a/solution.py
+++ b/solution.py
@@ -44,7 +44,8 @@
     image_next,
     resid_image,
     own_part,
-    field,
+    field_low,
+    field_high,
     field_ahead,
     col_out,
     row_out,
@@ -81,6 +82,7 @@
     has_behind = t > 0
     has_ahead = t < tiles - 1
 
+    fields = (field_low, field_high)
     loads = [
         pltpu.make_async_copy(right_hbm, right, in_sem.at[0]),
         pltpu.make_async_copy(order_hbm, order, in_sem.at[1]),
@@ -180,10 +182,10 @@
     def put_field(k, values, h):
         for b in range(blk_dev):
             at = b * block + h * LANES
-            field[k, h, s * blk_dev + b] = values[:, at : at + LANES].astype(BF16)
+            fields[h][k, s * blk_dev + b] = values[:, at : at + LANES].astype(BF16)
 
     def whole(k, q):
-        return jnp.concatenate([field[k, 0, q], field[k, 1, q]], axis=1)
+        return jnp.concatenate([field_low[k, q], field_high[k, q]], axis=1)
 
     def remote(src, dst, send, recv, target):
         return pltpu.make_async_remote_copy(
@@ -199,12 +201,12 @@
     sources = (across, below, above)
 
     def field_copy(k, row, h, n):
-        part = field.at[k, h, pl.ds(row * blk_dev, blk_dev)]
+        part = fields[h].at[k, pl.ds(row * blk_dev, blk_dev)]
         return remote(part, part, field_send.at[k], field_recv.at[k, h, n], (t, targets[n]))
 
     def ahead_copy(k, h, to):
         return remote(
-            field.at[k, h, pl.ds(0, blk_dev)],
+            fields[h].at[k, pl.ds(0, blk_dev)],
             field_ahead.at[k, h],
             ahead_send.at[k],
             ahead_recv.at[k],
@@ -232,11 +234,10 @@
             field_copy(k, s, h, n).start()
         pass_back(k, s, h)
 
-    def finish_field(k):
+    def finish_field(k, h):
         for n in (1, 2, 0):
-            for h in range(2):
-                field_copy(k, sources[n], h, n).wait_recv()
-                pass_back(k, sources[n], h)
+            field_copy(k, sources[n], h, n).wait_recv()
+            pass_back(k, sources[n], h)
 
     def finish_ahead(k):
         @pl.when(has_ahead)
@@ -245,7 +246,7 @@
 
         for h in range(2):
             for b in range(blk_dev):
-                field[k, h, subs * blk_dev + b] = field_ahead[k, h, b]
+                fields[h][k, subs * blk_dev + b] = field_ahead[k, h, b]
 
     def drain_field(k):
         sent = parts_out.at[k]
@@ -257,7 +258,7 @@
 
         @pl.when((s == 0) & far_behind)
         def _():
-            sent = field.at[k, :, pl.ds(0, subs * blk_dev)]
+            sent = field_low.at[pl.ds(0, 2), pl.ds(0, subs * blk_dev)]
             remote(sent, sent, ahead_send.at[k], ahead_recv.at[k], (t, above)).wait_send()
 
     def sums_start(k, stage, values):
@@ -392,27 +393,42 @@
     def dot(left, right_block, dims):
         return lax.dot_general(left, right_block, dims, preferred_element_type=F32)
 
-    def col_products(k, low, also=()):
+    def early_cols(k, low, also=()):
+        for u in range(middle):
+            p = low + u
+            left = field_low[k, table[9, p]]
+            col_out[1 + p] = dot(left, blocks[table[8, p], :LANES], across_rows)
+            if u % 2 == 0 and u // 2 < len(also):
+                turn(also[u // 2])
+
+    def col_products(k, low):
         total = jnp.zeros((rhs, block), F32)
         for u in range(middle):
             p = low + u
-            out = dot(whole(k, table[9, p]), blocks[table[8, p]], across_rows)
+            left = field_high[k, table[9, p]]
+            out = col_out[1 + p] + dot(left, blocks[table[8, p], LANES:], across_rows)
             col_out[1 + p] = out
             if k == ITERS - 1 and low > 0:
                 total = total + out * whole(k, table[10, p]).astype(F32)
-            if u % 2 == 0 and u // 2 < len(also):
-                turn(also[u // 2])
         return total
 
-    def row_products(k, low, is_turned, line, also=()):
+    def early_rows(k):
+        for p in range(middle, slots):
+            left = field_low[k, table[10, p]]
+            row_out[1 + p] = dot(left, turned[p, :LANES], across_rows)
+
+    def row_products(k, low, is_turned, line, is_early, also=()):
         share = tile_blocks // 2
         for u in range(middle):
             p = low + u
-            left = whole(k, table[10, p])
-            if is_turned(p):
-                row_out[1 + p] = dot(left, turned[p], across_rows)
+            if is_early:
+                left = field_high[k, table[10, p]]
+                out = row_out[1 + p] + dot(left, turned[p, LANES:], across_rows)
+            elif is_turned(p):
+                out = dot(whole(k, table[10, p]), turned[p], across_rows)
             else:
-                row_out[1 + p] = dot(left, blocks[table[8, p]], across_cols)
+                out = dot(whole(k, table[10, p]), blocks[table[8, p]], across_cols)
+            row_out[1 + p] = out
             if u < share:
                 q = line * share + u
                 half_sums[q] = listed_sum(col_out, 0, q, range(4))
@@ -544,16 +560,22 @@
         diag_products(0)
     pltpu.make_async_copy(blocks_hbm, blocks, blocks_sem).wait()
     with scope("finish0"):
-        finish_field(0)
+        finish_field(0, 0)
+    with scope("early0"):
+        quarter = middle // 2
+        early_cols(0, 0, range(middle, middle + quarter))
+        early_cols(0, middle, range(middle + quarter, slots))
+        early_rows(0)
+    with scope("finish0b"):
+        finish_field(0, 1)
     with scope("cols0"):
-        quarter = middle // 2
-        col_products(0, 0, range(middle, middle + quarter))
+        col_products(0, 0)
         send_ahead(0)
-        col_products(0, middle, range(middle + quarter, slots))
+        col_products(0, middle)
     with scope("rows0"):
-        row_products(0, middle, lambda p: True, 0, range(quarter))
+        row_products(0, middle, lambda p: True, 0, True, range(quarter))
         finish_ahead(0)
-        row_products(0, 0, lambda p: p < quarter, 1, range(quarter, middle))
+        row_products(0, 0, lambda p: p < quarter, 1, False, range(quarter, middle))
     with scope("send0"):
         send_products(0)
     with scope("own0"):
@@ -575,7 +597,13 @@
     with scope("diag1"):
         diag_products(1)
     with scope("finish1"):
-        finish_field(1)
+        finish_field(1, 0)
+    with scope("early1"):
+        early_cols(1, 0)
+        early_cols(1, middle)
+        early_rows(1)
+    with scope("finish1b"):
+        finish_field(1, 1)
     with scope("sums0b"):
         sums_start(0, 1, sums_finish(0, 0))
     with scope("cols1"):
@@ -583,10 +611,10 @@
         send_ahead(1)
         col_products(1, middle)
     with scope("rows1"):
-        row_products(1, middle, lambda p: True, 0)
+        row_products(1, middle, lambda p: True, 0, True)
     with scope("rows1b"):
         finish_ahead(1)
-        row_products(1, 0, lambda p: True, 1)
+        row_products(1, 0, lambda p: True, 1, False)
     with scope("send1"):
         send_products(1)
     with scope("sums0c"):
@@ -635,7 +663,12 @@
         w_now = image[...]
         local = fold(w_now * (own_part[...] + noise[...] * w_now))
     with scope("finish2"):
-        finish_field(2)
+        finish_field(2, 0)
+    with scope("early2"):
+        early_cols(2, 0)
+        early_cols(2, middle)
+    with scope("finish2b"):
+        finish_field(2, 1)
     with scope("sums1b"):
         sums_start(1, 1, sums_finish(1, 0))
     with scope("cols2"):
@@ -646,9 +679,9 @@
     with scope("sums2"):
         sums_start(2, 0, pack(local + 2.0 * quadratic(2, total)))
     with scope("rows2"):
-        row_products(2, middle, lambda p: True, 0)
+        row_products(2, middle, lambda p: True, 0, False)
     with scope("rows2b"):
-        row_products(2, 0, lambda p: True, 1)
+        row_products(2, 0, lambda p: True, 1, False)
     with scope("send2"):
         send_products(2)
     with scope("sums2b"):
@@ -728,7 +761,8 @@
                 vec,
                 vec,
                 vec,
-                pltpu.VMEM((ITERS, 2, (subs + 1) * blk_dev, rhs, LANES), BF16),
+                pltpu.VMEM((ITERS, (subs + 1) * blk_dev, rhs, LANES), BF16),
+                pltpu.VMEM((ITERS, (subs + 1) * blk_dev, rhs, LANES), BF16),
                 pltpu.VMEM((ITERS, 2, blk_dev, rhs, LANES), BF16),
                 pltpu.VMEM((1 + slots, rhs, block), F32),
                 pltpu.VMEM((1 + slots, rhs, block), F32),

time: 54.8 us -> 55.2 us (level)
  no operation moved by 1% of the time
where the time goes in v5:
time: 55.2 us; the launch traced here: 55.1 us
  Pallas kernels  53.2 us (96%)
  local copies, waits for them, and re-layouts  1.31 us (2%)
  between operations  0.64 us (1%)
    pallas_call x1, Pallas kernels, on_device(): pl.pallas_call(functools.partial(kernel, cfg), out_shape=(jax.ShapeDtypeS...  53.2 us
    unnamed x2, local copies, waits for them, and re-layouts  1.31 us

profile of v5, /device:TPU:0, one launch (start us, length us, event | category | flops | bytes accessed | tf_op | source)
XLA Modules:
  0.0 55.1 jit_solution(13045734246380036334)
XLA Ops:
  0.6 53.2 %block_pair_solve.1 = (f32[8,4096]{1,0:T(8,128)S(1)}, f32[8,4096]{1,0:T(8,128)S(1)}) custom-call(f32[8,4096]{1,0:T(8,128)} %right_hbm.1, s32[1,4096]{1,0:T(1,128)} %order_hbm.1, f32[1,4096]{1,0:T(1,128)} %bitcast.2, s32[2,96]{1,0:T(2,128)} %bitcast.3, bf16[96,256,256]{2,1,0:T(8,128)(2,1)} %blocks_hbm.1, bf16[16,256,256]{2,1,0:T(8,128)(2,1)} %diag_hbm.1), custom_call_target="tpu_custom_call" | custom-call | tf_op jit(solution)/shard_map/block_pair_solve/pallas_call | solution.py:744
  53.8 0.7 %copy.10 = f32[8,4096]{1,0:T(8,128)} copy(f32[8,4096]{1,0:T(8,128)S(1)} %get-tuple-element.4) | data formatting | bytes 262144
  54.5 0.7 %copy.11 = f32[8,4096]{1,0:T(8,128)} copy(f32[8,4096]{1,0:T(8,128)S(1)} %get-tuple-element.5) | data formatting | bytes 262144

commit v6 on v5

--- a/solution.py
+++ b/solution.py
@@ -76,9 +76,9 @@
     t = lax.axis_index("tile")
     s = lax.axis_index("sub")
     core = lax.rem(t, 2)
-    above = lax.rem(s + 1, subs)
-    below = lax.rem(s + subs - 1, subs)
-    across = lax.rem(s + 2, subs)
+    above = jnp.where(s == subs - 1, 0, s + 1)
+    below = jnp.where(s == 0, subs - 1, s - 1)
+    across = jnp.where(s >= subs - 2, s + 2 - subs, s + 2)
     has_behind = t > 0
     has_ahead = t < tiles - 1
 
@@ -99,68 +99,69 @@
         )
         for i in range(PARTS)
     ]
-    for copy in loads[:2]:
+    for copy in loads[:3]:
         copy.start()
+
+    def wrap(index, count):
+        return jnp.where(index >= count, index - count, index)
 
     group = core * subs + s
     chip_x = lax.rem(t // 2, side)
     chip_y = t // (2 * side)
-
-    def column_partner(index):
-        return (t - core + index // subs, lax.rem(index, subs))
-
-    def x_partner(index):
-        return ((chip_y * side + index) * 2 + core, s)
-
-    def y_partner(index):
-        return ((index * side + chip_x) * 2 + core, s)
-
-    def plane_partner(index):
-        return (index * 2 + core, s)
+    far_ahead = (core == 1) & has_ahead
+    far_behind = (core == 0) & has_behind
+    other_core = t + 1 - 2 * core
+    column = [(t, wrap(s + j, subs)) for j in range(1, subs)] + [
+        (other_core, wrap(s + j, subs)) for j in range(subs)
+    ]
+    along_x = [((chip_y * side + wrap(chip_x + j, side)) * 2 + core, s) for j in range(1, side)]
+    along_y = [((wrap(chip_y + j, side) * side + chip_x) * 2 + core, s) for j in range(1, side)]
+    plane = []
+    for i in range(side):
+        for j in range(side):
+            if i or j:
+                at = wrap(chip_y + i, side) * side + wrap(chip_x + j, side)
+                plane.append((at * 2 + core, s))
 
     stages = (
-        (2 * subs, group, column_partner, 0),
-        (side, chip_x, x_partner, 2 * subs),
-        (side, chip_y, y_partner, 2 * subs + side),
+        (group, column, 0),
+        (chip_x, along_x, 2 * subs),
+        (chip_y, along_y, 2 * subs + side),
     )
-    last_stages = (stages[0], (tiles // 2, t // 2, plane_partner, 2 * subs))
+    last_stages = (stages[0], (t // 2, plane, 2 * subs))
 
     def stages_of(k):
         return last_stages if k == ITERS - 1 else stages
 
     barrier = pltpu.get_barrier_semaphore()
-    greeted = 0
-    for count, mine, partner, unused in stages:
-        for j in range(1, count):
-            pl.semaphore_signal(
-                barrier, inc=1, device_id=partner(lax.rem(mine + j, count)), device_id_type=MESH
-            )
-            greeted += 1
-    far_ahead = (core == 1) & has_ahead
-    far_behind = (core == 0) & has_behind
+
+    def greet(target):
+        pl.semaphore_signal(barrier, inc=1, device_id=target, device_id_type=MESH)
 
     @pl.when(far_ahead)
     def _():
-        pl.semaphore_signal(barrier, inc=1, device_id=(t + 1, s), device_id_type=MESH)
-
         @pl.when(s > 0)
         def _():
-            pl.semaphore_signal(barrier, inc=1, device_id=(t + 1, 0), device_id_type=MESH)
+            greet((t + 1, 0))
+
+        greet((t + 1, s))
 
     @pl.when(far_behind)
     def _():
-        pl.semaphore_signal(barrier, inc=1, device_id=(t - 1, s), device_id_type=MESH)
-
         @pl.when(s == 0)
         def _():
             for j in range(1, subs):
-                pl.semaphore_signal(barrier, inc=1, device_id=(t - 1, j), device_id_type=MESH)
-
-    for copy in block_loads[:1]:
-        copy.start()
-    for copy in loads[2:]:
-        copy.start()
-    for copy in block_loads[1:]:
+                greet((t - 1, j))
+
+        greet((t - 1, s))
+
+    greeted = 0
+    for unused, members, also_unused in stages:
+        for target in members:
+            greet(target)
+            greeted += 1
+
+    for copy in (loads[4], *block_loads, loads[3]):
         copy.start()
 
     chunks = right.shape[1] // LANES
@@ -262,30 +263,24 @@
             remote(sent, sent, ahead_send.at[k], ahead_recv.at[k], (t, above)).wait_send()
 
     def sums_start(k, stage, values):
-        count, mine, partner, offset = stages_of(k)[stage]
+        mine, members, offset = stages_of(k)[stage]
         sums[k, offset + mine] = values
         own = sums.at[k, offset + mine]
-        for j in range(1, count):
-            remote(
-                own,
-                own,
-                sums_send.at[k, stage],
-                sums_recv.at[k, stage],
-                partner(lax.rem(mine + j, count)),
-            ).start()
+        for target in members:
+            remote(own, own, sums_send.at[k, stage], sums_recv.at[k, stage], target).start()
 
     def sums_waits(k, stage):
-        count, mine, partner, offset = stages_of(k)[stage]
-        others = sums.at[k, pl.ds(offset, count - 1)]
+        mine, members, offset = stages_of(k)[stage]
+        others = sums.at[k, pl.ds(offset, len(members))]
         return remote(
             others, others, sums_send.at[k, stage], sums_recv.at[k, stage], (t, above)
         )
 
     def sums_finish(k, stage):
-        count, mine, partner, offset = stages_of(k)[stage]
+        mine, members, offset = stages_of(k)[stage]
         sums_waits(k, stage).wait_recv()
         total = sums[k, offset]
-        for j in range(1, count):
+        for j in range(1, len(members) + 1):
             total = total + sums[k, offset + j]
         return total
 
@@ -376,8 +371,11 @@
 
     def listed_sum(out, line, q, kinds):
         at = q * 4
-        row = line + at // LANES
-        lane = lax.rem(at, LANES)
+        if isinstance(q, int):
+            row, lane = line + at // LANES, at % LANES
+        else:
+            row = line + lax.shift_right_logical(at, 7)
+            lane = lax.bitwise_and(at, LANES - 1)
         parts = [out[table[row, lane + n]] for n in kinds]
         while len(parts) > 1:
             paired = [x + y for x, y in zip(parts[::2], parts[1::2])]

time: 55.2 us -> 54.7 us (level)
  Pallas kernels: 53.2 us -> 52.6 us
where the time goes in v6:
time: 54.7 us; the launch traced here: 54.6 us
  Pallas kernels  52.6 us (96%)
  local copies, waits for them, and re-layouts  1.31 us (2%)
  between operations  0.64 us (1%)
    pallas_call x1, Pallas kernels, on_device(): pl.pallas_call(functools.partial(kernel, cfg), out_shape=(jax.ShapeDtypeS...  52.6 us
    unnamed x2, local copies, waits for them, and re-layouts  1.31 us

profile of v6, /device:TPU:0, one launch (start us, length us, event | category | flops | bytes accessed | tf_op | source)
XLA Modules:
  0.0 54.6 jit_solution(4519323564371720970)
XLA Ops:
  0.6 52.6 %block_pair_solve.1 = (f32[8,4096]{1,0:T(8,128)S(1)}, f32[8,4096]{1,0:T(8,128)S(1)}) custom-call(f32[8,4096]{1,0:T(8,128)} %right_hbm.1, s32[1,4096]{1,0:T(1,128)} %order_hbm.1, f32[1,4096]{1,0:T(1,128)} %bitcast.2, s32[2,96]{1,0:T(2,128)} %bitcast.3, bf16[96,256,256]{2,1,0:T(8,128)(2,1)} %blocks_hbm.1, bf16[16,256,256]{2,1,0:T(8,128)(2,1)} %diag_hbm.1), custom_call_target="tpu_custom_call" | custom-call | tf_op jit(solution)/shard_map/block_pair_solve/pallas_call | solution.py:742
  53.3 0.7 %copy.10 = f32[8,4096]{1,0:T(8,128)} copy(f32[8,4096]{1,0:T(8,128)S(1)} %get-tuple-element.4) | data formatting | bytes 262144
  53.9 0.7 %copy.11 = f32[8,4096]{1,0:T(8,128)} copy(f32[8,4096]{1,0:T(8,128)S(1)} %get-tuple-element.5) | data formatting | bytes 262144

commit v7 on v6

--- a/solution.py
+++ b/solution.py
@@ -99,7 +99,7 @@
         )
         for i in range(PARTS)
     ]
-    for copy in loads[:3]:
+    for copy in (*loads[:3], loads[4], *block_loads, loads[3]):
         copy.start()
 
     def wrap(index, count):
@@ -161,8 +161,6 @@
             greet(target)
             greeted += 1
 
-    for copy in (loads[4], *block_loads, loads[3]):
-        copy.start()
 
     chunks = right.shape[1] // LANES
 

time: 54.7 us -> 53.7 us (0.982)
  Pallas kernels: 52.6 us -> 51.7 us
    pallas_call x1, Pallas kernels: 52.6 us -> 51.7 us  [on_device(): pl.pallas_call(functools.partial(kernel, cfg), out_shape=(jax.ShapeDtypeS...]
where the time goes in v7:
time: 53.7 us; the launch traced here: 53.6 us
  Pallas kernels  51.7 us (96%)
  local copies, waits for them, and re-layouts  1.31 us (2%)
  between operations  0.64 us (1%)
    pallas_call x1, Pallas kernels, on_device(): pl.pallas_call(functools.partial(kernel, cfg), out_shape=(jax.ShapeDtypeS...  51.7 us
    unnamed x2, local copies, waits for them, and re-layouts  1.31 us

profile of v7, /device:TPU:0, one launch (start us, length us, event | category | flops | bytes accessed | tf_op | source)
XLA Modules:
  0.0 53.6 jit_solution(5912114515685484936)
XLA Ops:
  0.6 51.7 %block_pair_solve.1 = (f32[8,4096]{1,0:T(8,128)S(1)}, f32[8,4096]{1,0:T(8,128)S(1)}) custom-call(f32[8,4096]{1,0:T(8,128)} %right_hbm.1, s32[1,4096]{1,0:T(1,128)} %order_hbm.1, f32[1,4096]{1,0:T(1,128)} %bitcast.2, s32[2,96]{1,0:T(2,128)} %bitcast.3, bf16[96,256,256]{2,1,0:T(8,128)(2,1)} %blocks_hbm.1, bf16[16,256,256]{2,1,0:T(8,128)(2,1)} %diag_hbm.1), custom_call_target="tpu_custom_call" | custom-call | tf_op jit(solution)/shard_map/block_pair_solve/pallas_call | solution.py:740
  52.3 0.7 %copy.10 = f32[8,4096]{1,0:T(8,128)} copy(f32[8,4096]{1,0:T(8,128)S(1)} %get-tuple-element.4) | data formatting | bytes 262144
  53.0 0.7 %copy.11 = f32[8,4096]{1,0:T(8,128)} copy(f32[8,4096]{1,0:T(8,128)S(1)} %get-tuple-element.5) | data formatting | bytes 262144
